TPU v7x, 256 devices: a whole 4x4x8 slice. The times are simulated.
256 devices in a mesh: grp: 8 (over y, x_lo), ctx: 32 (over z, x_hi, core).
Axes of the slice: x: 4 (x_hi: 2, x_lo: 2; x = x_hi * 2 + x_lo), y: 4, z: 8, core: 2. Of those that a mesh axis runs over, the one named last changes fastest.
Arguments:
- tokens: bfloat16 [8, 2048, 4096], P('grp', 'ctx'), may hold values from -8 to 8
- req_lengths: int32 [8, 8], replicated, may hold values from 1 to 1088, 2048 in all within a row
- req_adapter: int32 [8, 8], replicated, may hold values from 0 to 7
- adapter_slot: int32 [8], replicated, may hold values from 0 to 7, each once
- query_weight: bfloat16 [4096, 4096], P(None, 'grp'), may hold values from -0.109375 to 0.109375
- key_weight: bfloat16 [4096, 1024], P(None, 'grp'), may hold values from -0.109375 to 0.109375
- value_weight: bfloat16 [4096, 1024], P(None, 'grp'), may hold values from -0.09375 to 0.09375
- w_out: bfloat16 [4096, 4096], P('grp'), may hold values from -0.09375 to 0.09375
- down_qkv: bfloat16 [8, 48, 4096], P('grp'), may hold values from -0.09375 to 0.09375
- up_query: bfloat16 [8, 16, 4096], P('grp'), may hold values from -0.59765625 to 0.59765625
- up_kv: bfloat16 [8, 2, 16, 1024], P('grp'), may hold values from -0.59765625 to 0.59765625
- down_out: bfloat16 [8, 16, 4096], P('grp'), may hold values from -0.09375 to 0.09375
- up_out: bfloat16 [8, 16, 4096], P('grp'), may hold values from -0.59765625 to 0.59765625
Outputs:
- mixed: bfloat16 [8, 2048, 4096], P('grp', 'ctx')
Inputs may be any that keep to these rules, and one draw needn't show every extreme that they name: `req_lengths`: row b holds the lengths of group b's 8 requests in order; each row sums to 2048 and its longest request has 1088 positions. adapter a's tables stand at slot adapter_slot[a]; every slot is used by one adapter.
All inputs are finite; a program needn't handle non-finite values.
Results may differ from a plain program's by a relative error of at most 0.015.
The roundings to bfloat16 on the way count: a program that leaves them out, or rounds other values in their place, can miss the bound.
Values may be sent and summed in bfloat16 or wider, within the bound.
A program may use at most 128 MiB of HBM per device.

v0:
```python
import math

import jax
import jax.numpy as jnp
from jax import lax
from jax.sharding import PartitionSpec as P

MODEL_WIDTH = 4096
HD = 128
ADAPTER_RANK = 16


ROPE_BASE = 500000.0
ADAPTER_SCALE = 2.0
MASKED_SCORE = -1e30


def request_info(lengths, adapter_ids, positions):
    req_ends = jnp.cumsum(lengths, axis=-1)
    starts = req_ends - lengths
    segment = jnp.sum((req_ends[..., None, :] <= positions[:, None]).astype(jnp.int32), axis=-1)
    req_picks = (segment[..., None] == jnp.arange(lengths.shape[-1], dtype=jnp.int32)).astype(
        jnp.int32
    )
    req_begin = jnp.sum(req_picks * starts[..., None, :], axis=-1)
    req_owner = jnp.sum(req_picks * adapter_ids[..., None, :], axis=-1)
    return (segment, req_begin, req_owner)


def rotate(values, offsets):
    half_width = values.shape[-1] // 2
    frequency = jnp.exp(
        jnp.arange(half_width, dtype=jnp.float32) * (-2.0 * math.log(ROPE_BASE) / values.shape[-1])
    )
    angles = offsets[..., None, None] * frequency
    cosine = jnp.cos(angles)
    sine = jnp.sin(angles)
    lower_half = values[..., :half_width]
    upper_half = values[..., half_width:]
    return jnp.concatenate(
        [lower_half * cosine - upper_half * sine, upper_half * cosine + lower_half * sine], axis=-1
    )


def widen_rows(adapter_middle, adapter_onehot, upward_table):
    masked_scores = adapter_onehot[:, :, None] * adapter_middle[:, None, :]
    flat_rows = masked_scores.reshape(
        masked_scores.shape[0], upward_table.shape[0] * upward_table.shape[1]
    )
    return jnp.dot(
        flat_rows,
        upward_table.reshape(upward_table.shape[0] * upward_table.shape[1], upward_table.shape[2]),
        preferred_element_type=jnp.float32,
    )


def narrow_rows(input_rows, down_table, adapter_onehot):
    every_term = jnp.einsum(
        "gtd,afd->gtaf", input_rows, down_table, preferred_element_type=jnp.float32
    )
    return jnp.sum(every_term * adapter_onehot[..., None].astype(jnp.float32), axis=2).astype(
        jnp.bfloat16
    )


def body(
    tokens,
    req_lengths,
    req_adapter,
    adapter_slot,
    query_weight,
    key_weight,
    value_weight,
    w_out,
    down_qkv,
    up_query,
    up_kv,
    down_out,
    up_out,
):
    groups = req_lengths.shape[0]
    token_matrix = tokens.shape[1]
    adapters = adapter_slot.shape[0]
    group_index = lax.axis_index("grp")
    block_index = lax.axis_index("ctx")
    q_cols = query_weight.shape[1]
    kv_cols = key_weight.shape[1]
    kv_local = kv_cols // HD
    heads_per_kv = q_cols // kv_cols
    positions = block_index * token_matrix + jnp.arange(token_matrix, dtype=jnp.int32)
    seg_rows, begin_rows, owner_rows = request_info(req_lengths, req_adapter, positions)
    onehot_rows = (owner_rows[..., None] == jnp.arange(adapters, dtype=jnp.int32)).astype(
        jnp.bfloat16
    )
    own_hot = lax.dynamic_slice_in_dim(onehot_rows, group_index, 1, 0)
    down_slots, upq_slots, upkv_slots, downo_slots, upo_slots = (
        lax.all_gather(down_qkv, "grp", axis=0, tiled=True),
        lax.all_gather(up_query, "grp", axis=0, tiled=True),
        lax.all_gather(up_kv, "grp", axis=0, tiled=True),
        lax.all_gather(down_out, "grp", axis=0, tiled=True),
        lax.all_gather(up_out, "grp", axis=0, tiled=True),
    )
    upq_slots = lax.dynamic_slice_in_dim(upq_slots, group_index * q_cols, q_cols, 2)
    upkv_slots = lax.dynamic_slice_in_dim(upkv_slots, group_index * kv_cols, kv_cols, 3)
    downo_slots = lax.dynamic_slice_in_dim(downo_slots, group_index * q_cols, q_cols, 2)
    down_adapter = jnp.take(down_slots, adapter_slot, axis=0)
    up_query_adapter = jnp.take(upq_slots, adapter_slot, axis=0)
    up_key_value_adapter = jnp.take(upkv_slots, adapter_slot, axis=0)
    downo_ad = jnp.take(downo_slots, adapter_slot, axis=0)
    up_output_adapter = jnp.take(upo_slots, adapter_slot, axis=0)
    all_requests = lax.all_gather(tokens, "grp", axis=0, tiled=True)
    adapter_middle = narrow_rows(all_requests, down_adapter, onehot_rows)
    count_of_rows = groups * token_matrix
    flat_inputs = all_requests.reshape(count_of_rows, MODEL_WIDTH)
    onehot_flat = onehot_rows.reshape(count_of_rows, adapters)
    middle_flat = adapter_middle.reshape(count_of_rows, 3 * ADAPTER_RANK)
    offsets = (positions[None, :] - begin_rows).astype(jnp.float32).reshape(count_of_rows)
    query_total = jnp.dot(
        flat_inputs, query_weight, preferred_element_type=jnp.float32
    ) + ADAPTER_SCALE * widen_rows(middle_flat[:, 0:ADAPTER_RANK], onehot_flat, up_query_adapter)
    key_total = jnp.dot(
        flat_inputs, key_weight, preferred_element_type=jnp.float32
    ) + ADAPTER_SCALE * widen_rows(
        middle_flat[:, ADAPTER_RANK : 2 * ADAPTER_RANK], onehot_flat, up_key_value_adapter[:, 0]
    )
    value_total = jnp.dot(
        flat_inputs, value_weight, preferred_element_type=jnp.float32
    ) + ADAPTER_SCALE * widen_rows(
        middle_flat[:, 2 * ADAPTER_RANK : 3 * ADAPTER_RANK], onehot_flat, up_key_value_adapter[:, 1]
    )
    query = rotate(query_total.reshape(count_of_rows, q_cols // HD, HD), offsets).astype(
        jnp.bfloat16
    )
    query = query.reshape(groups, token_matrix, kv_local, heads_per_kv, HD)
    key = (
        rotate(key_total.reshape(count_of_rows, kv_local, HD), offsets)
        .astype(jnp.bfloat16)
        .reshape(groups, token_matrix, kv_cols)
    )
    value = value_total.astype(jnp.bfloat16).reshape(groups, token_matrix, kv_cols)
    score_scale = math.sqrt(HD)
    start_top = jnp.full((groups, token_matrix, kv_local, heads_per_kv), MASKED_SCORE, jnp.float32)
    key_piece = lax.all_gather(key, "ctx", axis=1, tiled=True)
    value_piece = lax.all_gather(value, "ctx", axis=1, tiled=True)
    key_count = key_piece.shape[1]
    key_positions = jnp.arange(key_count, dtype=jnp.int32)
    key_segment, unused_begin, unused_owner = request_info(req_lengths, req_adapter, key_positions)
    allowed = (
        (key_segment[:, None, :] == seg_rows[:, :, None])
        & (key_positions[None, None, :] <= positions[None, :, None])
        & (key_positions[None, None, :] >= 0)
    )
    key_heads = key_piece.reshape(groups, key_count, kv_local, HD)
    value_heads = value_piece.reshape(groups, key_count, kv_local, HD)
    scores = (
        jnp.einsum("gtkjd,gskd->gtkjs", query, key_heads, preferred_element_type=jnp.float32)
        / score_scale
    )
    mask_full = allowed[:, :, None, None, :]
    scores = jnp.where(mask_full, scores, MASKED_SCORE)
    new_top = jnp.maximum(start_top, jnp.max(scores, axis=-1))
    weights = jnp.where(mask_full, jnp.exp(scores - new_top[..., None]), 0.0)
    new_sum = jnp.sum(weights, axis=-1)
    new_accum = jnp.einsum(
        "gtkjs,gskd->gtkjd",
        weights.astype(jnp.bfloat16),
        value_heads,
        preferred_element_type=jnp.float32,
    )
    final_state = (new_top, new_sum, new_accum)
    final_top, final_sum, final_accum = final_state
    attended = (
        (final_accum / final_sum[..., None])
        .astype(jnp.bfloat16)
        .reshape(groups, token_matrix, q_cols)
    )
    attended_flat = attended.reshape(count_of_rows, q_cols)
    mid_terms = jnp.einsum(
        "pc,arc->par", attended_flat, downo_ad, preferred_element_type=jnp.float32
    )
    out_terms = jnp.sum(mid_terms * onehot_flat[..., None].astype(jnp.float32), axis=1).reshape(
        groups, token_matrix, ADAPTER_RANK
    )
    output_middle = lax.psum_scatter(
        out_terms.astype(jnp.bfloat16), "grp", scatter_dimension=0, tiled=True
    )
    partial_term = jnp.einsum("gtc,cd->gtd", attended, w_out, preferred_element_type=jnp.float32)
    base_product = lax.psum_scatter(
        lax.optimization_barrier(partial_term.astype(jnp.bfloat16))
        .astype(jnp.float32)
        .astype(jnp.bfloat16),
        "grp",
        scatter_dimension=0,
        tiled=True,
    ).astype(jnp.float32)
    adapter_delta = widen_rows(
        output_middle.reshape(token_matrix, ADAPTER_RANK),
        own_hot.reshape(token_matrix, adapters),
        up_output_adapter,
    )
    return (
        base_product + ADAPTER_SCALE * adapter_delta.reshape(1, token_matrix, MODEL_WIDTH)
    ).astype(jnp.bfloat16)


def solution(mesh):
    placed = (
        P("grp", "ctx", None),
        P(),
        P(),
        P(),
        P(None, "grp"),
        P(None, "grp"),
        P(None, "grp"),
        P("grp", None),
        P("grp", None, None),
        P("grp", None, None),
        P("grp", None, None, None),
        P("grp", None, None),
        P("grp", None, None),
    )
    return jax.shard_map(
        body, mesh=mesh, in_specs=placed, out_specs=P("grp", "ctx", None), check_vma=False
    )
```

profile of v0, /device:TPU:2, one launch (start us, length us, event | category | flops | bytes accessed | tf_op | source)
XLA Modules:
  0.0 637.0 jit_solution(13202051979169333373)
XLA Ops:
  6.5 0.7 all-gather.10.cloned.1.call-update
  7.3 0.7 all-gather.8.cloned.1.call-update
  8.1 0.7 all-gather.16.cloned.1.call-update
  8.8 0.5 all-gather.18.cloned.1.call-update
  9.4 0.7 compare_select_fusion
  10.0 0.7 compare_and_fusion.1
  10.7 0.8 reduce_window_sum.12
  11.5 0.7 sub.31
  12.2 0.1 convert_reduce_fusion.1
  12.3 0.8 select_reduce_fusion
  13.1 0.1 eq.66
  13.3 33.0 %all_gather.26 = bf16[8,2,16,1024]{3,2,1,0:T(8,128)(2,1)S(1)} all-gather(bf16[1,2,16,1024]{3,2,1,0:T(8,128)(2,1)} %param.25), channel_id=1, replica_groups=mesh['grp'=8,'ctx'=32] {'grp'}, dimensions={0}, use_global_device_ids=true | all-gather | bytes 589824 | tf_op jit(solution)/shard_map/all_gather | solution.py:99
  46.3 0.6 gather_fusion.1
  46.8 0.1 broadcast_select_fusion
  46.9 0.1 convert_element_type.102
  47.0 43.9 %all-gather.10.cloned.1.call-done = bf16[8,48,4096]{2,1,0:T(8,128)(2,1)} async-done(((bf16[1,48,4096]{2,1,0:T(8,128)(2,1)}), bf16[8,48,4096]{2,1,0:T(8,128)(2,1)}) %all-gather.10.cloned.1.call-update) | async-done | bytes 3145744 | tf_op jit(solution)/shard_map/all_gather | solution.py:97
  91.0 4.3 gather_fusion
  95.3 91.5 %all-gather.8.cloned.1.call-done = bf16[8,64,4096]{2,1,0:T(8,128)(2,1)} async-done(((bf16[1,64,4096]{2,1,0:T(8,128)(2,1)}), bf16[8,64,4096]{2,1,0:T(8,128)(2,1)}) %all-gather.8.cloned.1.call-update) | async-done | bytes 4194320 | tf_op jit(solution)/shard_map/all_gather | solution.py:111
  186.7 6.2 fusion.20
  193.0 0.1 convert_element_type.98
  193.2 3.5 fusion.88
  196.7 0.2 fusion.30
  197.0 1.2 fusion.58
  198.2 0.8 pad_maximum_fusion
  199.0 0.0 all-gather.12.cloned.1.call-start
  199.0 3.5 fusion.87
  202.5 0.9 fusion.32
  203.4 0.0 all-gather.20.cloned.1.call-start
  203.5 0.7 all-gather.20.cloned.1.call-update
  204.2 0.5 multiply_cosine_fusion.1
  204.8 0.1 iota_compare_fusion
  204.9 0.2 convert_reduce_fusion
  205.1 0.8 compare_and_fusion
  205.9 24.4 %all-gather.16.cloned.1.call-done = bf16[8,16,4096]{2,1,0:T(8,128)(2,1)} async-done(((bf16[1,16,4096]{2,1,0:T(8,128)(2,1)}), bf16[8,16,4096]{2,1,0:T(8,128)(2,1)}) %all-gather.16.cloned.1.call-update) | async-done | bytes 1048592 | tf_op jit(solution)/shard_map/all_gather | solution.py:98
  230.3 0.9 constant_dynamic-slice_fusion
  231.3 0.6 gather_fusion.3
  231.8 42.3 %all-gather.18.cloned.1.call-done = bf16[8,16,4096]{2,1,0:T(8,128)(2,1)} async-done(((bf16[1,16,4096]{2,1,0:T(8,128)(2,1)}), bf16[8,16,4096]{2,1,0:T(8,128)(2,1)}) %all-gather.18.cloned.1.call-update) | async-done | bytes 1048592 | tf_op jit(solution)/shard_map/all_gather | solution.py:100
  274.2 0.9 constant_dynamic-slice_fusion.2
  275.1 0.6 gather_fusion.4
  275.6 5.8 fusion.89
  281.5 0.4 fusion.28
  281.9 0.2 subtract_convert_fusion
  282.1 0.3 concatenate.24
  282.4 0.4 copy.51
  282.8 0.3 concatenate.25
  283.1 0.4 copy.52
  283.5 80.5 %all-gather.14.cloned.1.call-done = bf16[8,2048,128]{2,1,0:T(8,128)(2,1)} async-done(((bf16[8,64,128]{2,1,0:T(8,128)(2,1)}), bf16[8,2048,128]{2,1,0:T(8,128)(2,1)}) %all-gather.14.cloned.1.call-update) | async-done | bytes 4194320 | tf_op jit(solution)/shard_map/all_gather | solution.py:143
  364.0 10.0 %fusion = (f32[8,64,4]{1,2,0:T(4,128)S(1)}, f32[8,2048,64,4]{1,2,3,0:T(8,128)}) fusion(pred[8,64,2048]{2,1,0:T(8,128)(4,1)S(1)} %compare_and_fusion, bf16[8,64,4,64]{3,1,2,0:T(8,128)(2,1)S(1)} %copy.52, bf16[8,64,4,64]{3,1,2,0:T(8,128)(2,1)S(1)} %copy.51, bf16[8,2048,128]{2,1,0:T(8,128)(2,1)} %all-gather.14.cloned.1.call-done), kind=kOutput, calls=%fused_computation.7 | convolution fusion | flops 1087371264 | bytes 22552576 | tf_op jit(solution)/shard_map/gtkjd,gskd->gtkjs/dot_general | solution.py:156
  374.0 8.6 %fusion.1 = f32[8,64,4]{1,2,0:T(4,128)S(1)} fusion(f32[8,2048,64,4]{1,2,3,0:T(8,128)} %get-tuple-element.26, f32[8,64,4]{1,2,0:T(4,128)S(1)} %broadcast_maximum_fusion, pred[8,64,2048]{2,1,0:T(8,128)(4,1)S(1)} %compare_and_fusion), kind=kLoop, calls=%fused_computation.8 | loop fusion | flops 20969472 | bytes 17842176 | tf_op jit(solution)/shard_map/reduce_sum | solution.py:163
  382.6 67.5 %all-gather.12.cloned.1.call-done = bf16[8,2048,128]{2,1,0:T(8,128)(2,1)} async-done(((bf16[8,64,128]{2,1,0:T(8,128)(2,1)}), bf16[8,2048,128]{2,1,0:T(8,128)(2,1)}) %all-gather.12.cloned.1.call-update) | async-done | bytes 4194320 | tf_op jit(solution)/shard_map/all_gather | solution.py:144
  450.1 9.8 %fusion.44 = bf16[8,64,1,4,128]{4,1,3,0,2:T(8,128)(2,1)S(1)} fusion(f32[8,2048,64,4]{1,2,3,0:T(8,128)} %get-tuple-element.26, f32[8,64,4]{1,2,0:T(4,128)S(1)} %broadcast_maximum_fusion, pred[8,64,2048]{2,1,0:T(8,128)(4,1)S(1)} %compare_and_fusion, bf16[8,2048,128]{2,1,0:T(8,128)(2,1)} %all-gather.12.cloned.1.call-done, f32[8,64,4]{1,2,0:T(4,128)S(1)} %fusion.1), kind=kOutput, calls=%fused_computation.47 | convolution fusion | flops 1095237632 | bytes 22560768 | tf_op jit(solution)/shard_map/gtkjs,gskd->gtkjd/dot_general | solution.py:164
  459.8 0.4 copy.53
  460.3 0.2 reshape.328
  460.5 0.2 reshape.384
  460.7 0.3 fusion.33
  461.0 0.1 convert_element_type.110
  461.1 0.6 copy.55
  461.7 0.0 reduce-scatter.3.cloned.1.call-start
  461.8 6.5 %convolution_convert_fusion = bf16[8,64,4096]{2,1,0:T(8,128)(2,1)} fusion(bf16[8,64,512]{2,1,0:T(8,128)(2,1)S(1)} %reshape.328, bf16[512,4096]{1,0:T(8,128)(2,1)} %param.22), kind=kOutput, calls=%fused_computation.13 | convolution fusion | flops 2149580800 | bytes 8912896 | tf_op jit(solution)/shard_map/gtc,cd->gtd/dot_general | solution.py:187
  468.3 21.8 %all-gather.20.cloned.1.call-done = bf16[8,16,4096]{2,1,0:T(8,128)(2,1)} async-done(((bf16[1,16,4096]{2,1,0:T(8,128)(2,1)}), bf16[8,16,4096]{2,1,0:T(8,128)(2,1)}) %all-gather.20.cloned.1.call-update) | async-done | bytes 1048592 | tf_op jit(solution)/shard_map/all_gather | solution.py:101
  490.1 1.8 gather_fusion.2
  491.9 39.5 %reduce-scatter.5.cloned.1.call-done = bf16[1,64,16]{1,2,0:T(8,128)(2,1)} async-done(((bf16[8,64,16]{1,2,0:T(8,128)(2,1)}), bf16[1,64,16]{1,2,0:T(8,128)(2,1)}) %reduce-scatter.5.cloned.1.call-update) | async-done | bytes 2064 | tf_op jit(solution)/shard_map/reduce_scatter | solution.py:184
  531.4 96.8 %reduce-scatter.3.cloned.1.call-done = bf16[1,64,4096]{2,1,0:T(8,128)(2,1)} async-done(((bf16[8,64,4096]{2,1,0:T(8,128)(2,1)}), bf16[1,64,4096]{2,1,0:T(8,128)(2,1)}) %reduce-scatter.3.cloned.1.call-update) | async-done | bytes 524304 | tf_op jit(solution)/shard_map/reduce_scatter | solution.py:188
  628.3 2.2 fusion.10
  (30 shorter events, 0.4 us)
Async XLA Ops:
  6.5 186.7 %copy-start = (bf16[4096,128]{1,0:T(8,128)(2,1)S(1)}, bf16[4096,128]{1,0:T(8,128)(2,1)}, u32[]{:S(2)}) copy-start(bf16[4096,128]{1,0:T(8,128)(2,1)} %param.20) | copy-start | bytes 3145732
  6.5 84.4 %all-gather.10.cloned.1.call-start = ((), (), s32[]{:S(2)}) async-start(), calls=%async_computation.3 | async-start | bytes 3538944 | tf_op jit(solution)/shard_map/all_gather | solution.py:97
  7.3 179.5 %all-gather.8.cloned.1.call-start = ((), (), s32[]{:S(2)}) async-start(), calls=%async_computation.2 | async-start | bytes 4718592 | tf_op jit(solution)/shard_map/all_gather | solution.py:111
  8.0 222.3 %all-gather.16.cloned.1.call-start = ((), (), s32[]{:S(2)}) async-start(), calls=%async_computation.6 | async-start | bytes 1179648 | tf_op jit(solution)/shard_map/all_gather | solution.py:98
  8.7 265.4 %all-gather.18.cloned.1.call-start = ((), (), s32[]{:S(2)}) async-start(), calls=%async_computation.8 | async-start | bytes 1179648 | tf_op jit(solution)/shard_map/all_gather | solution.py:100
  9.3 354.7 %all-gather.14.cloned.1.call-start = ((), (), s32[]{:S(2)}) async-start(), calls=%async_computation.5 | async-start | bytes 4325376 | tf_op jit(solution)/shard_map/all_gather | solution.py:143
  193.0 6.0 copy-start.2
  199.0 251.1 %all-gather.12.cloned.1.call-start = ((), (), s32[]{:S(2)}) async-start(), calls=%async_computation.4 | async-start | bytes 4325376 | tf_op jit(solution)/shard_map/all_gather | solution.py:144
  203.4 286.7 %all-gather.20.cloned.1.call-start = ((), (), s32[]{:S(2)}) async-start(), calls=%async_computation.10 | async-start | bytes 1179648 | tf_op jit(solution)/shard_map/all_gather | solution.py:101
  204.2 327.3 %reduce-scatter.5.cloned.1.call-start = ((), (), s32[]{:S(2)}) async-start(), calls=%async_computation.9 | async-start | bytes 36864 | tf_op jit(solution)/shard_map/reduce_scatter | solution.py:184
  461.7 166.5 %reduce-scatter.3.cloned.1.call-start = ((), (), s32[]{:S(2)}) async-start(), calls=%async_computation.7 | async-start | bytes 4718592 | tf_op jit(solution)/shard_map/reduce_scatter | solution.py:188
  468.3 162.2 %copy-start.1 = (bf16[4096,128]{1,0:T(8,128)(2,1)S(1)}, bf16[4096,128]{1,0:T(8,128)(2,1)}, u32[]{:S(2)}) copy-start(bf16[4096,128]{1,0:T(8,128)(2,1)} %param.20) | copy-start | bytes 3145732
Sparse Core Ops, SparseCore 0:
  9.1 81.7 all-gather.9
  92.7 93.9 all-gather.7
  188.5 41.7 all-gather.15
  232.0 42.1 all-gather.17
  276.8 87.1 all-gather.13
  366.7 83.2 all-gather.11
  451.9 38.1 all-gather.19
  492.6 38.8 reduce-scatter.4
  534.0 94.2 reduce-scatter.2
where the time goes:
time: 639 us; the launch traced here: 637 us
  waiting for transfers between devices  512 us (80%)
  matrix products  49.3 us (8%)
  blocking collectives  33 us (5%)
  other arithmetic  16.3 us (3%)
  between operations  13.5 us (2%)
  local copies, waits for them, and re-layouts  13 us (2%)
    reduce_scatter x1, waiting for transfers between devices, body(): lax.psum_scatter(lax.optimization_barrier(partial_term.astype(jnp.bfloat1...  96.8 us
    all_gather x1, waiting for transfers between devices, body(): all_requests = lax.all_gather(tokens, 'grp', axis=0, tiled=True)  91.5 us
    all_gather x1, waiting for transfers between devices, body(): key_piece = lax.all_gather(key, 'ctx', axis=1, tiled=True)  80.5 us
    all_gather x1, waiting for transfers between devices, body(): value_piece = lax.all_gather(value, 'ctx', axis=1, tiled=True)  67.5 us
    all_gather x1, waiting for transfers between devices, body(): lax.all_gather(down_qkv, 'grp', axis=0, tiled=True)  43.9 us
    all_gather x1, waiting for transfers between devices, body(): lax.all_gather(down_out, 'grp', axis=0, tiled=True)  42.3 us
    reduce_scatter x1, waiting for transfers between devices, body(): lax.psum_scatter(out_terms.astype(jnp.bfloat16), 'grp', scatter_dimension...  39.5 us
    all_gather x1, blocking collectives, body(): lax.all_gather(up_kv, 'grp', axis=0, tiled=True)  33 us
  transfers between devices with their start and end apart: 9, of which 9 were waited for; matrix products, arithmetic and copies ran while one was open for 12% of the time, Pallas kernels for 0%

commit v1 on v0

v1 whole, which is shorter than its diff:
```python
import functools
import math

import jax
import jax.numpy as jnp
import numpy as np
from jax import lax
from jax.experimental import pallas as pl
from jax.experimental.pallas import tpu as pltpu
from jax.sharding import PartitionSpec as P

D = 4096
HD = 128
RK = 16
REQS = 8
ROPE_BASE = 500000.0
MESH = pl.DeviceIdType.MESH
F32 = jnp.float32
BF16 = jnp.bfloat16
NEG = -1e30

QC = 512
KVC = 128
HR = 32
KCH = 1024
NCH = D // KCH
NJ = 2 * NCH
LEAD = 3


class Place:
    def __init__(self):
        self.g = lax.axis_index("grp")
        self.c = lax.axis_index("ctx")
        self.y = self.g // 2
        self.xl = self.g % 2
        self.z = self.c // 4
        self.xh = (self.c // 2) % 2
        self.co = self.c % 2
        self.xh2 = (self.xh + self.co) % 2

    def group(self, dy, flip):
        return ((self.y + dy) % 4) * 2 + (self.xl + flip) % 2

    def peer(self, dy, flip):
        ctx = self.z * 4 + self.xh2 * 2 + self.co if flip else self.c
        return (self.group(dy, flip), ctx)

    def level(self, z):
        return (self.g, z * 4 + self.xh * 2 + self.co)

    def quarter(self, b):
        xh = jnp.where((b % 2) == self.xl, self.xh, self.xh2)
        return xh * 2 + self.co


PEERS = [(dy, flip) for dy in range(4) for flip in range(2)][1:]


def rcopy(src, dst, ssem, rsem, device):
    return pltpu.make_async_remote_copy(
        src_ref=src, dst_ref=dst, send_sem=ssem, recv_sem=rsem, device_id=device, device_id_type=MESH
    )


def greet(devices):
    barrier = pltpu.get_barrier_semaphore()
    for device in devices:
        pl.semaphore_signal(barrier, inc=1, device_id=device, device_id_type=MESH)
    pl.semaphore_wait(barrier, len(devices))


def row_slots(place, half, lens, adap, aslot):
    lane = lax.broadcasted_iota(jnp.int32, (8, 256), 1)
    out = jnp.zeros((8, 256), jnp.int32)
    for b in range(8):
        pos = 64 * (place.z * 4 + place.quarter(b)) + HR * half + lane - b * HR
        mine = (lane >= b * HR) & (lane < (b + 1) * HR)
        end = jnp.int32(0)
        for r in range(REQS):
            begin = end
            end = begin + lens[b, r]
            hit = mine & (pos >= begin) & (pos < end)
            out = jnp.where(hit, aslot[adap[b, r]], out)
    return out


def front_kernel(
    lens, adap, aslot, tok, wq, wk, wv, dn, uq, ukv, freq,
    q_out, kv_out,
    xall, w, acc, accm, uq_all, uk_all, uv_all, midsend, mid_all, qbuf, kvbuf, cosb, sinb,
    lsem, tsem_s, tsem_r, ss, rr, ms, mr, zs, zr, gs, gr, osem,
):
    pc = Place()
    z = pc.z
    partner = pc.peer(0, 1)
    up = pc.peer(1, 0)
    down = pc.peer(3, 0)
    mate = (pc.g, z * 4 + pc.xh * 2 + 1 - pc.co)
    across = (pc.g, z * 4 + (1 - pc.xh) * 2 + pc.co)

    loads = [
        pltpu.make_async_copy(wq, w.at[:, 0:QC], lsem.at[0]),
        pltpu.make_async_copy(wk, w.at[:, QC : QC + KVC], lsem.at[1]),
        pltpu.make_async_copy(wv, w.at[:, QC + KVC : QC + 2 * KVC], lsem.at[2]),
        pltpu.make_async_copy(tok.at[0:HR, :], xall.at[0, pc.g], lsem.at[3]),
        pltpu.make_async_copy(tok.at[HR : 2 * HR, :], xall.at[1, pc.g], lsem.at[4]),
    ]
    for load in loads:
        load.start()

    greet(
        [pc.peer(*p) for p in PEERS]
        + [pc.level((z + d) % 8) for d in range(1, 8)]
        + [mate, across]
    )

    def part(J):
        return J // NCH, pl.ds(pl.multiple_of((J % NCH) * KCH, KCH), KCH)

    def block(J, group):
        h, cols = part(J)
        return xall.at[h, group, :, cols]

    def own_copies(J):
        h, cols = part(J)
        src = tok.at[pl.ds(pl.multiple_of(h * HR, HR), HR), cols]
        dst = block(J, pc.g)
        return (
            rcopy(src, dst, ss.at[J, 0], rr.at[J, 2], up),
            rcopy(src, dst, ss.at[J, 1], rr.at[J, 3], down),
            rcopy(src, dst, ss.at[J, 2], rr.at[J, 1], partner),
        )

    def forward(J, slot, group, ssem, rslot, device):
        ref = block(J, group)
        return rcopy(ref, ref, ss.at[J, ssem], rr.at[J, rslot], device)

    g_dn, g_up, g_far = pc.group(3, 0), pc.group(1, 0), pc.group(2, 0)

    def waiting(J, slot, group):
        ref = block(J, group)
        return rcopy(ref, ref, ss.at[J, 0], rr.at[J, slot], partner)

    def own(J):
        for copy in own_copies(J):
            copy.start()

    def stage_a(J):
        waiting(J, 2, g_dn).wait_recv()
        forward(J, 2, g_dn, 3, 4, partner).start()

        @pl.when(J % 2 == 0)
        def _():
            forward(J, 2, g_dn, 6, 6, up).start()

        waiting(J, 3, g_up).wait_recv()
        forward(J, 3, g_up, 4, 5, partner).start()

        @pl.when(J % 2 == 1)
        def _():
            forward(J, 3, g_up, 6, 6, down).start()

    def stage_b(J):
        waiting(J, 6, g_far).wait_recv()
        forward(J, 6, g_far, 5, 7, partner).start()

    def stage_c(J):
        for slot, dy in ((1, 0), (4, 3), (5, 1), (7, 2)):
            waiting(J, slot, pc.group(dy, 1)).wait_recv()
        h, cols = part(J)
        x = xall[h, :, :, cols].reshape(8 * HR, KCH)

        @pl.when(J % NCH == 0)
        def _():
            acc[h] = jnp.zeros(acc.shape[1:], F32)
            accm[h] = jnp.zeros(accm.shape[1:], F32)

        rows = pl.ds(pl.multiple_of((J % NCH) * KCH, KCH), KCH)
        accm[h] += lax.dot_general(
            dn[:, cols], x, (((1,), (1,)), ((), ())), preferred_element_type=F32
        )
        acc[h] += jnp.dot(x, w[rows, :], preferred_element_type=F32)

    def step(t, carry=None):
        @pl.when(t + LEAD < NJ)
        def _():
            own(t + LEAD)

        @pl.when(t < NJ)
        def _():
            stage_a(t)

        @pl.when((t >= 1) & (t < NJ + 1))
        def _():
            stage_b(t - 1)

        @pl.when(t >= 2)
        def _():
            stage_c(t - 2)

        return carry

    for J in range(LEAD):
        own(J)

    def table_copies(k, dy, flip):
        device = pc.peer(dy, flip)
        i = pc.group(dy, flip)
        qcols = pl.ds(pl.multiple_of(i * QC, QC), QC)
        kcols = pl.ds(pl.multiple_of(i * KVC, KVC), KVC)
        return (
            rcopy(uq.at[:, qcols], uq_all.at[pc.g], tsem_s.at[k, 0], tsem_r.at[k, 0], device),
            rcopy(ukv.at[0, :, kcols], uk_all.at[pc.g], tsem_s.at[k, 1], tsem_r.at[k, 1], device),
            rcopy(ukv.at[1, :, kcols], uv_all.at[pc.g], tsem_s.at[k, 2], tsem_r.at[k, 2], device),
        )

    for k, (dy, flip) in enumerate(PEERS):
        for copy in table_copies(k, dy, flip):
            copy.start()
    qcols = pl.ds(pl.multiple_of(pc.g * QC, QC), QC)
    kcols = pl.ds(pl.multiple_of(pc.g * KVC, KVC), KVC)
    uq_all[pc.g] = uq[:, qcols]
    uk_all[pc.g] = ukv[0, :, kcols]
    uv_all[pc.g] = ukv[1, :, kcols]

    sub = lax.broadcasted_iota(jnp.int32, (HR, HD), 0)
    low = lax.broadcasted_iota(jnp.int32, (HR, HD), 1) < HD // 2
    for half in range(2):
        for b in range(8):
            pos = 64 * (z * 4 + pc.quarter(b)) + HR * half + sub
            begin = jnp.zeros((HR, HD), jnp.int32)
            end = jnp.int32(0)
            for r in range(REQS):
                length = lens[b, r]
                end = end + length
                begin = begin + jnp.where(pos >= end, length, 0)
            angle = (pos - begin).astype(F32) * freq[...]
            rows = pl.ds(half * 256 + b * HR, HR)
            cosb[rows, :] = jnp.cos(angle)
            sine = jnp.sin(angle)
            sinb[rows, :] = jnp.where(low, -sine, sine)

    for load in loads:
        load.wait()

    def mid_copies(half):
        return [
            rcopy(midsend.at[half], mid_all.at[half, pc.g], ms.at[half, k], mr.at[half, k], pc.peer(*p))
            for k, p in enumerate(PEERS)
        ]

    def finish_mid(half):
        keep = (row_slots(pc, half, lens, adap, aslot)[0:1, :] == pc.g).astype(F32)
        mid = (accm[half] * keep).astype(BF16).reshape(3, RK, 256)
        midsend[half] = mid
        mid_all[half, pc.g] = mid
        for copy in mid_copies(half):
            copy.start()

    def z_copies(half, d):
        zd = (z + d) % 8
        quarter = pc.quarter(zd)
        return (
            rcopy(kvbuf.at[half, zd], kv_out.at[z, quarter, half], zs.at[half, d, 1], zr.at[half, d, 1], pc.level(zd)),
            rcopy(qbuf.at[half, zd], q_out.at[z, half], zs.at[half, d, 0], zr.at[half, d, 0], pc.level(zd)),
        )

    def own_out(half):
        return (
            pltpu.make_async_copy(kvbuf.at[half, z], kv_out.at[z, pc.quarter(z), half], osem.at[half, 1]),
            pltpu.make_async_copy(qbuf.at[half, z], q_out.at[z, half], osem.at[half, 0]),
        )

    def finish_rows(half):
        for copy in mid_copies(half):
            copy.wait_recv()
        rows = pl.ds(half * 256, 256)
        cosv, sinv = cosb[rows, :], sinb[rows, :]

        def widen(which, table, base):
            mid = mid_all[half, :, which].reshape(8 * RK, 256)
            n = table.shape[2]
            delta = lax.dot_general(
                mid, table[...].reshape(8 * RK, n), (((0,), (0,)), ((), ())), preferred_element_type=F32
            )
            return base + 2.0 * delta

        def rope(v):
            return v * cosv + pltpu.roll(v, HD // 2, 1) * sinv

        query = widen(0, uq_all, acc[half, :, 0:QC])
        for j in range(4):
            qbuf[half, :, :, j * HD : (j + 1) * HD] = (
                rope(query[:, j * HD : (j + 1) * HD]).astype(BF16).reshape(8, HR, HD)
            )
        key = rope(widen(1, uk_all, acc[half, :, QC : QC + KVC]))
        kvbuf[half, :, :, 0:HD] = key.astype(BF16).reshape(8, HR, HD)
        value = widen(2, uv_all, acc[half, :, QC + KVC : QC + 2 * KVC])
        kvbuf[half, :, :, HD : 2 * HD] = value.astype(BF16).reshape(8, HR, HD)
        for d in (4, 3, 5, 2, 6, 1, 7):
            for copy in z_copies(half, d):
                copy.start()
        for copy in own_out(half):
            copy.start()

    q_own = pc.quarter(z)
    q_across = (1 - q_own // 2) * 2 + pc.co
    xh_mate = jnp.where((z % 2) == pc.xl, pc.xh, (pc.xh + 1 - pc.co) % 2)
    q_mate = xh_mate * 2 + 1 - pc.co
    q_mate_across = (1 - xh_mate) * 2 + 1 - pc.co

    def column(quarter, half):
        return kv_out.at[:, quarter, half]

    def kv_copy(quarter, half, k, device):
        ref = column(quarter, half)
        return rcopy(ref, ref, gs.at[half, k], gr.at[half, k], device)

    def spread_own(half):
        for copy in own_out(half):
            copy.wait()
        for d in range(1, 8):
            z_copies(half, d)[0].wait_recv()
        kv_copy(q_own, half, 1, across).start()
        kv_copy(q_own, half, 0, mate).start()

    def spread_across(half):
        kv_copy(q_across, half, 1, across).wait_recv()
        kv_copy(q_across, half, 2, mate).start()

    lax.fori_loop(0, NCH + 2, step, None)
    for k, (dy, flip) in enumerate(PEERS):
        for copy in table_copies(k, dy, flip):
            copy.wait_recv()
    finish_mid(0)
    lax.fori_loop(NCH + 2, NJ, step, None)
    finish_rows(0)
    lax.fori_loop(NJ, NJ + 2, step, None)
    finish_mid(1)
    spread_own(0)
    finish_rows(1)
    spread_across(0)
    spread_own(1)
    spread_across(1)

    for half in range(2):
        kv_copy(q_mate, half, 0, mate).wait_recv()
        kv_copy(q_mate_across, half, 2, mate).wait_recv()
        for d in range(1, 8):
            kv, q = z_copies(half, d)
            q.wait_recv()
            kv.wait_send()
            q.wait_send()
        kv_copy(q_own, half, 1, across).wait_send()
        kv_copy(q_own, half, 0, mate).wait_send()
        kv_copy(q_across, half, 2, mate).wait_send()
        for copy in mid_copies(half):
            copy.wait_send()
    for k, (dy, flip) in enumerate(PEERS):
        for copy in table_copies(k, dy, flip):
            copy.wait_send()

    def drain(J, carry):
        for copy in own_copies(J):
            copy.wait_send()
        for k in range(3, 7):
            forward(J, 0, pc.g, k, 0, partner).wait_send()
        return carry

    lax.fori_loop(0, NJ, drain, None)


def front(lens, adap, aslot, tok, wq, wk, wv, dn, uq, ukv, freq):
    any_ = pl.BlockSpec(memory_space=pl.ANY)
    vmem = pl.BlockSpec(memory_space=pltpu.VMEM)
    smem = pl.BlockSpec(memory_space=pltpu.SMEM)
    dma = pltpu.SemaphoreType.DMA
    return pl.pallas_call(
        front_kernel,
        name="front",
        out_shape=(
            jax.ShapeDtypeStruct((8, 2, HR, QC), BF16),
            jax.ShapeDtypeStruct((8, 4, 2, HR, 2 * HD), BF16),
        ),
        in_specs=[smem] * 3 + [any_] * 4 + [vmem] * 4,
        out_specs=(any_, any_),
        scratch_shapes=[
            pltpu.VMEM((2, 8, HR, D), BF16),
            pltpu.VMEM((D, QC + 2 * KVC), BF16),
            pltpu.VMEM((2, 256, QC + 2 * KVC), F32),
            pltpu.VMEM((2, 3 * RK, 256), F32),
            pltpu.VMEM((8, RK, QC), BF16),
            pltpu.VMEM((8, RK, KVC), BF16),
            pltpu.VMEM((8, RK, KVC), BF16),
            pltpu.VMEM((2, 3, RK, 256), BF16),
            pltpu.VMEM((2, 8, 3, RK, 256), BF16),
            pltpu.VMEM((2, 8, HR, QC), BF16),
            pltpu.VMEM((2, 8, HR, 2 * HD), BF16),
            pltpu.VMEM((512, HD), F32),
            pltpu.VMEM((512, HD), F32),
            dma((5,)),
            dma((7, 3)),
            dma((7, 3)),
            dma((NJ, 7)),
            dma((NJ, 8)),
            dma((2, 7)),
            dma((2, 7)),
            dma((2, 8, 2)),
            dma((2, 8, 2)),
            dma((2, 3)),
            dma((2, 3)),
            dma((2, 2)),
        ],
        compiler_params=pltpu.CompilerParams(
            collective_id=0, has_side_effects=True, vmem_limit_bytes=60 << 20
        ),
    )(lens, adap, aslot, tok, wq, wk, wv, dn, uq, ukv, freq)


CK = 256


def attend_kernel(lens, q_ref, kv_ref, o_ref):
    pc = Place()
    z = pc.z
    zs = pl.program_id(0)
    quarter = pc.quarter(z)
    first = 64 * (zs * 4 + quarter)
    row = lax.broadcasted_iota(jnp.int32, (256, CK), 0) % 64
    col = lax.broadcasted_iota(jnp.int32, (256, CK), 1)
    pos = first + row
    begin = jnp.zeros((256, CK), jnp.int32)
    end = jnp.int32(0)
    head = jnp.int32(0)
    for r in range(REQS):
        length = lens[z, r]
        end = end + length
        begin = begin + jnp.where(pos >= end, length, 0)
        head = head + jnp.where(first >= end, length, 0)
    q = q_ref[...].reshape(64, QC)
    q = jnp.concatenate([q[:, j * HD : (j + 1) * HD] for j in range(4)], axis=0)
    scale = 1.0 / math.sqrt(HD)

    def chunk(j, state):
        top, total, accum = state
        keys = kv_ref[j, :, 0:HD]
        values = kv_ref[j, :, HD : 2 * HD]
        s = lax.dot_general(q, keys, (((1,), (1,)), ((), ())), preferred_element_type=F32) * scale
        at = j * CK + col
        kept = (at >= begin) & (at <= pos)
        s = jnp.where(kept, s, NEG)
        new = jnp.maximum(top, jnp.max(s, axis=1, keepdims=True))
        p = jnp.where(kept, jnp.exp(s - new), 0.0)
        fade = jnp.exp(top - new)
        total = total * fade + jnp.sum(p, axis=1, keepdims=True)
        accum = accum * fade + jnp.dot(p.astype(BF16), values, preferred_element_type=F32)
        return new, total, accum

    state = (
        jnp.full((256, 1), NEG, F32),
        jnp.zeros((256, 1), F32),
        jnp.zeros((256, HD), F32),
    )
    top, total, accum = lax.fori_loop(head // CK, zs + 1, chunk, state)
    out = (accum / total).astype(BF16)
    for j in range(4):
        o_ref[0, :, :, j * HD : (j + 1) * HD] = out[j * 64 : (j + 1) * 64].reshape(2, HR, HD)


def attend(lens, q, kv):
    return pl.pallas_call(
        attend_kernel,
        name="attend",
        grid=(8,),
        out_shape=jax.ShapeDtypeStruct((8, 2, HR, QC), BF16),
        in_specs=[
            pl.BlockSpec(memory_space=pltpu.SMEM),
            pl.BlockSpec((1, 2, HR, QC), lambda i: (i, 0, 0, 0)),
            pl.BlockSpec((8, 256, 2 * HD), lambda i: (0, 0, 0)),
        ],
        out_specs=pl.BlockSpec((1, 2, HR, QC), lambda i: (i, 0, 0, 0)),
        compiler_params=pltpu.CompilerParams(vmem_limit_bytes=40 << 20),
    )(lens, q, kv.reshape(8, 256, 2 * HD))


NC = 512
NN = D // NC
NT = 2 * NN


def back_kernel(
    lens, adap, aslot, att, w_out, do, uo,
    out,
    w, att_all, do_all, omsend, om_recv, om, pbuf, xrecv, sbuf, far, tup, tdn, rup, rdn,
    lsem, ds_s, ds_r, zs, zr, os_, or_, xs, xr, ys, yr, osem,
):
    pc = Place()
    z = pc.z
    partner = pc.peer(0, 1)
    up = pc.peer(1, 0)
    down = pc.peer(3, 0)

    load = pltpu.make_async_copy(w_out, w, lsem.at[0])
    load.start()
    own_att = [pltpu.make_async_copy(att.at[z, h], att_all.at[h, z], osem.at[h]) for h in range(2)]
    for copy in own_att:
        copy.start()
    own_do = pltpu.make_async_copy(
        do.at[:, pl.ds(pl.multiple_of(pc.g * QC, QC), QC)], do_all.at[pc.g], lsem.at[1]
    )
    own_do.start()

    greet([pc.peer(*p) for p in PEERS] + [pc.level((z + d) % 8) for d in range(1, 8)])

    def z_copy(half, d):
        zd = (z + d) % 8
        return rcopy(att.at[zd, half], att_all.at[half, z], zs.at[half, d], zr.at[half, d], pc.level(zd))

    for half in range(2):
        for d in (4, 3, 5, 2, 6, 1, 7):
            z_copy(half, d).start()

    def do_copy(k, dy, flip):
        i = pc.group(dy, flip)
        cols = pl.ds(pl.multiple_of(i * QC, QC), QC)
        return rcopy(do.at[:, cols], do_all.at[pc.g], ds_s.at[k], ds_r.at[k], pc.peer(dy, flip))

    for k, p in enumerate(PEERS):
        do_copy(k, *p).start()
    load.wait()
    own_do.wait()
    for k, p in enumerate(PEERS):
        do_copy(k, *p).wait_recv()

    def om_copy(half, k, dy, flip):
        i = pc.group(dy, flip)
        return rcopy(
            omsend.at[half, i], om_recv.at[half, pc.g], os_.at[half, k], or_.at[half, k], pc.peer(dy, flip)
        )

    def mid_send(half):
        own_att[half].wait()
        for d in range(1, 8):
            z_copy(half, d).wait_recv()
        rows = att_all[half].reshape(256, QC)
        mid = lax.dot_general(
            do_all[...].reshape(8 * RK, QC), rows, (((1,), (1,)), ((), ())), preferred_element_type=F32
        ).reshape(8, RK, 256)
        omsend[half] = mid
        for k, p in enumerate(PEERS):
            om_copy(half, k, *p).start()
        om_recv[half, pc.g] = omsend[half, pc.g]

    def mid_done(half):
        for k, p in enumerate(PEERS):
            om_copy(half, k, *p).wait_recv()
        keep = (row_slots(pc, half, lens, adap, aslot)[0:1, :] == pc.g).astype(F32)
        om[half] = (jnp.sum(om_recv[half], axis=0) * keep).astype(BF16)

    y_far, y_up, y_dn = (pc.y + 2) % 4, (pc.y + 1) % 4, (pc.y + 3) % 4

    def x_copy(J):
        return rcopy(pbuf.at[J, :, 1 - pc.xl], xrecv.at[J], xs.at[J], xr.at[J], partner)

    def far_copy(J, odd):
        device = down if odd else up
        return rcopy(sbuf.at[J, y_far], far.at[J], ys.at[J, 0], yr.at[J, 0], device)

    def up_copy(J):
        return rcopy(tup.at[J], rup.at[J], ys.at[J, 1], yr.at[J, 1], up)

    def dn_copy(J):
        return rcopy(tdn.at[J], rdn.at[J], ys.at[J, 2], yr.at[J, 2], down)

    def stage_p(J):
        half = J // NN
        cols = pl.ds(pl.multiple_of((J % NN) * NC, NC), NC)
        rows = att_all[half].reshape(256, QC)
        total = jnp.dot(rows, w[:, cols], preferred_element_type=F32) + 2.0 * lax.dot_general(
            om[half], uo[:, cols], (((0,), (0,)), ((), ())), preferred_element_type=F32
        )
        pbuf[J] = total.astype(BF16).reshape(4, 2, HR, NC)
        x_copy(J).start()

    def stage_s(J, odd):
        x_copy(J).wait_recv()
        total = pbuf[J, :, pc.xl].astype(F32) + xrecv[J].astype(F32)
        sbuf[J] = total.astype(BF16)
        far_copy(J, odd).start()
        if odd:
            tup[J] = sbuf[J, y_up]
            up_copy(J).start()
        else:
            tdn[J] = sbuf[J, y_dn]
            dn_copy(J).start()

    def stage_t(J, odd):
        far_copy(J, odd).wait_recv()
        if odd:
            tdn[J] = (sbuf[J, y_dn].astype(F32) + far[J].astype(F32)).astype(BF16)
            dn_copy(J).start()
        else:
            tup[J] = (sbuf[J, y_up].astype(F32) + far[J].astype(F32)).astype(BF16)
            up_copy(J).start()

    def stage_f(J):
        up_copy(J).wait_recv()
        dn_copy(J).wait_recv()
        half = J // NN
        cols = pl.ds(pl.multiple_of((J % NN) * NC, NC), NC)
        total = sbuf[J, pc.y].astype(F32) + rup[J].astype(F32) + rdn[J].astype(F32)
        out[pl.ds(pl.multiple_of(half * HR, HR), HR), cols] = total.astype(BF16)

    def step(t, carry=None):
        @pl.when(t < NT // 2)
        def _():
            stage_p(2 * t)
            stage_p(2 * t + 1)

        @pl.when((t >= 1) & (t < NT // 2 + 1))
        def _():
            stage_s(2 * t - 2, False)
            stage_s(2 * t - 1, True)

        @pl.when((t >= 2) & (t < NT // 2 + 2))
        def _():
            stage_t(2 * t - 4, False)
            stage_t(2 * t - 3, True)

        @pl.when(t >= 3)
        def _():
            stage_f(2 * t - 6)
            stage_f(2 * t - 5)

        return carry

    mid_send(0)
    mid_done(0)
    lax.fori_loop(0, 2, step, None)
    mid_send(1)
    lax.fori_loop(2, NN // 2, step, None)
    mid_done(1)
    lax.fori_loop(NN // 2, NT // 2 + 3, step, None)

    for half in range(2):
        for d in range(1, 8):
            z_copy(half, d).wait_send()
        for k, p in enumerate(PEERS):
            om_copy(half, k, *p).wait_send()
    for k, p in enumerate(PEERS):
        do_copy(k, *p).wait_send()

    def drain(J, carry):
        x_copy(J).wait_send()
        far_copy(J, False).wait_send()
        up_copy(J).wait_send()
        dn_copy(J).wait_send()
        return carry

    lax.fori_loop(0, NT, drain, None)


def back(lens, adap, aslot, att, w_out, do, uo):
    any_ = pl.BlockSpec(memory_space=pl.ANY)
    vmem = pl.BlockSpec(memory_space=pltpu.VMEM)
    smem = pl.BlockSpec(memory_space=pltpu.SMEM)
    dma = pltpu.SemaphoreType.DMA
    return pl.pallas_call(
        back_kernel,
        name="back",
        out_shape=jax.ShapeDtypeStruct((64, D), BF16),
        in_specs=[smem] * 3 + [any_] * 3 + [vmem],
        out_specs=vmem,
        scratch_shapes=[
            pltpu.VMEM((QC, D), BF16),
            pltpu.VMEM((2, 8, HR, QC), BF16),
            pltpu.VMEM((8, RK, QC), BF16),
            pltpu.VMEM((2, 8, RK, 256), F32),
            pltpu.VMEM((2, 8, RK, 256), F32),
            pltpu.VMEM((2, RK, 256), BF16),
            pltpu.VMEM((NT, 4, 2, HR, NC), BF16),
            pltpu.VMEM((NT, 4, HR, NC), BF16),
            pltpu.VMEM((NT, 4, HR, NC), BF16),
            pltpu.VMEM((NT, HR, NC), BF16),
            pltpu.VMEM((NT, HR, NC), BF16),
            pltpu.VMEM((NT, HR, NC), BF16),
            pltpu.VMEM((NT, HR, NC), BF16),
            pltpu.VMEM((NT, HR, NC), BF16),
            dma((2,)),
            dma((7,)),
            dma((7,)),
            dma((2, 8)),
            dma((2, 8)),
            dma((2, 7)),
            dma((2, 7)),
            dma((NT,)),
            dma((NT,)),
            dma((NT, 3)),
            dma((NT, 3)),
            dma((2,)),
        ],
        compiler_params=pltpu.CompilerParams(
            collective_id=1, has_side_effects=True, vmem_limit_bytes=60 << 20
        ),
    )(lens, adap, aslot, att, w_out, do, uo)


def body(
    tokens, req_lengths, req_adapter, adapter_slot, query_weight, key_weight, value_weight, w_out,
    down_qkv, up_query, up_kv, down_out, up_out,
):
    half = np.arange(HD) % (HD // 2)
    freq = jnp.asarray(np.exp(half * (-2.0 * math.log(ROPE_BASE) / HD)).astype(np.float32)[None, :])
    q, kv = front(
        req_lengths, req_adapter, adapter_slot, tokens[0], query_weight, key_weight, value_weight,
        down_qkv[0], up_query[0], up_kv[0], freq,
    )
    att = attend(req_lengths, q, kv)
    out = back(req_lengths, req_adapter, adapter_slot, att, w_out, down_out[0], up_out[0])
    return out[None]


def solution(mesh):
    placed = (
        P("grp", "ctx", None),
        P(),
        P(),
        P(),
        P(None, "grp"),
        P(None, "grp"),
        P(None, "grp"),
        P("grp", None),
        P("grp", None, None),
        P("grp", None, None),
        P("grp", None, None, None),
        P("grp", None, None),
        P("grp", None, None),
    )
    return jax.shard_map(
        body, mesh=mesh, in_specs=placed, out_specs=P("grp", "ctx", None), check_vma=False
    )
```

time: 639 us -> 142 us (0.22)
  waiting for transfers between devices: 512 us -> 0 us
  Pallas kernels: 0 us -> 137 us
  matrix products: 49.3 us -> 0 us
  blocking collectives: 33 us -> 0 us
  other arithmetic: 16.3 us -> 0 us
  between operations: 13.5 us -> 0.05 us
  local copies, waits for them, and re-layouts: 13 us -> 4.92 us
    all_gather x7 -> x0, waiting for transfers between devices: 372 us -> none  [the longest x1 91.5 us: body(): all_requests = lax.all_gather(tokens, 'grp', axis=0, tiled=True)]
    pallas_call x0 -> x3, Pallas kernels: none -> 137 us  [the longest x1 69.2 us: front(): pl.pallas_call(front_kernel, name='front', out_shape=(jax.ShapeDtypeStruc...]
    reduce_scatter x2 -> x0, waiting for transfers between devices: 136 us -> none  [the longest x1 96.8 us: body(): lax.psum_scatter(lax.optimization_barrier(partial_term.astype(jnp.bfloat1...]
    dot_general x12 -> x0, matrix products: 49.3 us -> none  [the longest x1 9.97 us: body(): jnp.einsum('gtkjd,gskd->gtkjs', query, key_heads, preferred_element_type=...]
    all_gather x1 -> x0, blocking collectives: 33 us -> none  [body(): lax.all_gather(up_kv, 'grp', axis=0, tiled=True)]
    reduce_sum x4 -> x0, other arithmetic: 9.69 us -> none  [the longest x1 8.58 us: body(): new_sum = jnp.sum(weights, axis=-1)]
    gather x5 -> x0, local copies, waits for them, and re-layouts: 7.85 us -> none  [the longest x1 4.34 us: body(): down_adapter = jnp.take(down_slots, adapter_slot, axis=0)]
  transfers between devices with their start and end apart: 9 -> 0, of which waited for: 9 -> 0; matrix products, arithmetic and copies ran while one was open for 12% -> 0% of each run, Pallas kernels for 0% -> 0%
where the time goes in v1:
time: 142 us
  Pallas kernels  137 us (96%)
  local copies, waits for them, and re-layouts  4.92 us (3%)
    pallas_call x1, Pallas kernels, front(): pl.pallas_call(front_kernel, name='front', out_shape=(jax.ShapeDtypeStruc...  69.2 us
    pallas_call x1, Pallas kernels, back(): pl.pallas_call(back_kernel, name='back', out_shape=jax.ShapeDtypeStruct((...  56.5 us
    pallas_call x1, Pallas kernels, attend(): pl.pallas_call(attend_kernel, name='attend', grid=(8,), out_shape=jax.Sha...  11.2 us
    unnamed x9, local copies, waits for them, and re-layouts  4.92 us

profile of v1, /device:TPU:2, one launch (start us, length us, event | category | flops | bytes accessed | tf_op | source)
XLA Modules:
  0.0 141.9 jit_solution(1453954881191276870)
XLA Ops:
  0.0 0.0 copy-start.3
  0.0 69.2 %front.1 = (bf16[8,2,32,512]{3,2,1,0:T(8,128)(2,1)}, bf16[8,4,2,32,256]{4,3,2,1,0:T(8,128)(2,1)}) custom-call(s32[8,8]{1,0:T(8,128)} %lens.5, s32[8,8]{1,0:T(8,128)} %adap.3, s32[8]{0:T(128)} %aslot.3, bf16[64,4096]{1,0:T(8,128)(2,1)} %bitcast.10, bf16[4096,512]{1,0:T(8,128)(2,1)} %wq.1, bf16[4096,128]{1,0:T(8,128)(2,1)} %wk.1, bf16[4096,128]{1,0:T(8,128)(2,1)} %wv.1, ...), custom_call_target="tpu_custom_call" | custom-call | tf_op jit(solution)/shard_map/front/pallas_call | solution.py:379
  69.2 0.0 copy-done.3
  69.2 0.0 copy-start.1
  69.2 1.2 copy-done.1
  70.4 0.0 copy-start.2
  70.4 1.0 copy-done.2
  71.5 11.2 %attend.1.att = bf16[8,2,32,512]{3,2,1,0:T(8,128)(2,1)S(1)} custom-call(s32[8,8]{1,0:T(8,128)S(1)} %copy-done.3, bf16[8,2,32,512]{3,2,1,0:T(8,128)(2,1)S(1)} %copy-done.2, bf16[8,256,256]{2,1,0:T(8,128)(2,1)S(1)} %bitcast.8), custom_call_target="tpu_custom_call" | custom-call | tf_op jit(solution)/shard_map/attend/pallas_call | solution.py:472
  82.7 0.0 copy-start
  82.7 0.8 copy-done
  83.5 56.5 %back.1 = bf16[64,4096]{1,0:T(8,128)(2,1)} custom-call(s32[8,8]{1,0:T(8,128)} %lens.5, s32[8,8]{1,0:T(8,128)} %adap.3, s32[8]{0:T(128)} %aslot.3, bf16[8,2,32,512]{3,2,1,0:T(8,128)(2,1)} %copy-done, bf16[512,4096]{1,0:T(8,128)(2,1)} %w_out.1, bf16[16,4096]{1,0:T(8,128)(2,1)} %bitcast.13, bf16[16,4096]{1,0:T(8,128)(2,1)} %bitcast.14), custom_call_target="tpu_custom_call" | custom-call | tf_op jit(solution)/shard_map/back/pallas_call | solution.py:669
  140.0 1.9 %copy.16 = bf16[1,64,4096]{2,1,0:T(8,128)(2,1)} copy(bf16[1,64,4096]{2,1,0:T(8,128)(2,1)} %bitcast.9) | data formatting | bytes 1048576
Async XLA Ops:
  0.0 69.2 %copy-start.3 = (s32[8,8]{1,0:T(8,128)S(1)}, s32[8,8]{1,0:T(8,128)}, u32[]{:S(2)}) copy-start(s32[8,8]{1,0:T(8,128)} %lens.5) | copy-start | bytes 772
  69.2 1.2 copy-start.1
  70.4 1.0 copy-start.2
  82.7 0.8 copy-start

commit v2 on v0

v2 whole, which is shorter than its diff:
```python
import functools
import math

import jax
import jax.numpy as jnp
import numpy as np
from jax import lax
from jax.experimental import pallas as pl
from jax.experimental.pallas import tpu as pltpu
from jax.sharding import PartitionSpec as P

D = 4096
HD = 128
RK = 16
REQS = 8
ROPE_BASE = 500000.0
MESH = pl.DeviceIdType.MESH
F32 = jnp.float32
BF16 = jnp.bfloat16
NEG = -1e30

QC = 512
KVC = 128
H = 4
HR = 64 // H
NR = 8 * HR
NCH = 4
KCH = D // NCH
NJ = H * NCH
LEAD = 5
LAG_B, LAG_C, LAG_ROWS, LAG_OWN, LAG_ACROSS = 2, 5, 7, 11, 13
BR = 32
CK = 384
NK = -(-(1088 + BR - 1) // CK)
NC = 512
NN = D // NC
NT = 2 * NN


class Place:
    def __init__(self):
        self.g = lax.axis_index("grp")
        self.c = lax.axis_index("ctx")
        self.y = self.g // 2
        self.xl = self.g % 2
        self.z = self.c // 4
        self.xh = (self.c // 2) % 2
        self.co = self.c % 2
        self.xh2 = (self.xh + self.co) % 2

    def group(self, dy, flip):
        return ((self.y + dy) % 4) * 2 + (self.xl + flip) % 2

    def peer(self, dy, flip):
        ctx = self.z * 4 + self.xh2 * 2 + self.co if flip else self.c
        return (self.group(dy, flip), ctx)

    def level(self, z):
        return (self.g, z * 4 + self.xh * 2 + self.co)

    def quarter(self, b):
        xh = jnp.where((b % 2) == self.xl, self.xh, self.xh2)
        return xh * 2 + self.co


PEERS = [(dy, flip) for dy in range(4) for flip in range(2)][1:]


def rcopy(src, dst, ssem, rsem, device):
    return pltpu.make_async_remote_copy(
        src_ref=src, dst_ref=dst, send_sem=ssem, recv_sem=rsem, device_id=device, device_id_type=MESH
    )


def greet(devices):
    barrier = pltpu.get_barrier_semaphore()
    for device in devices:
        pl.semaphore_signal(barrier, inc=1, device_id=device, device_id_type=MESH)
    pl.semaphore_wait(barrier, len(devices))


def row_slots(place, groups, rows, offset, lens, adap, aslot):
    lane = lax.broadcasted_iota(jnp.int32, (8, len(groups) * rows), 1)
    out = jnp.zeros(lane.shape, jnp.int32)
    for i, b in enumerate(groups):
        pos = 64 * (place.z * 4 + place.quarter(b)) + offset + lane - i * rows
        mine = (lane >= i * rows) & (lane < (i + 1) * rows)
        end = jnp.int32(0)
        for r in range(REQS):
            begin = end
            end = begin + lens[b, r]
            hit = mine & (pos >= begin) & (pos < end)
            out = jnp.where(hit, aslot[adap[b, r]], out)
    return out[0:1, :]


def layer_kernel(
    lens, adap, aslot, tok, wq, wk, wv, w_out, dn_hbm, uq, ukv, do, uo_hbm, freq,
    out,
    xall, w, wo, dn, uo, acc, accm, uq_all, uk_all, uv_all, do_all, midsend, mid_all, qbuf, kvbuf,
    cosb, sinb, q_all, kv_all, att_buf, att_all, omsend, om_recv, om, pbuf, xrecv, sbuf, far, tup, tdn, rup, rdn,
    lsem, ts, tr, ss, rr, ms, mr, zs_s, zs_r, gs, gr, as_, ar, os_, or_, xs, xr, ys, yr,
):
    pc = Place()
    z = pc.z
    partner = pc.peer(0, 1)
    up = pc.peer(1, 0)
    down = pc.peer(3, 0)
    mate = (pc.g, z * 4 + pc.xh * 2 + 1 - pc.co)
    across = (pc.g, z * 4 + (1 - pc.xh) * 2 + pc.co)
    qcols = pl.ds(pl.multiple_of(pc.g * QC, QC), QC)
    kcols = pl.ds(pl.multiple_of(pc.g * KVC, KVC), KVC)

    local = [
        (wq, w.at[:, 0:QC]),
        (wk, w.at[:, QC : QC + KVC]),
        (wv, w.at[:, QC + KVC : QC + 2 * KVC]),
        (dn_hbm, dn),
        (uq.at[:, qcols], uq_all.at[pc.g]),
        (ukv.at[0, :, kcols], uk_all.at[pc.g]),
        (ukv.at[1, :, kcols], uv_all.at[pc.g]),
        (do.at[:, qcols], do_all.at[pc.g]),
    ] + [(tok.at[h * HR : (h + 1) * HR, :], xall.at[h, pc.g]) for h in range(H)] + [
        (uo_hbm, uo.at[pc.xl]),
        (w_out, wo),
    ]
    loads = [pltpu.make_async_copy(src, dst, lsem.at[i]) for i, (src, dst) in enumerate(local)]
    for load in loads:
        load.start()

    greet(
        [pc.peer(*p) for p in PEERS]
        + [pc.level((z + d) % 8) for d in range(1, 8)]
        + [mate, across]
    )

    def part(J):
        return J // NCH, pl.ds(pl.multiple_of((J % NCH) * KCH, KCH), KCH)

    def block(J, group):
        h, cols = part(J)
        return xall.at[h, group, :, cols]

    def own_copies(J):
        h, cols = part(J)
        src = tok.at[pl.ds(pl.multiple_of(h * HR, HR), HR), cols]
        dst = block(J, pc.g)
        return (
            rcopy(src, dst, ss.at[J, 0], rr.at[J, 2], up),
            rcopy(src, dst, ss.at[J, 1], rr.at[J, 3], down),
            rcopy(src, dst, ss.at[J, 2], rr.at[J, 1], partner),
        )

    def forward(J, group, ssem, rslot, device):
        ref = block(J, group)
        return rcopy(ref, ref, ss.at[J, ssem], rr.at[J, rslot], device)

    def arrived(J, slot, group):
        ref = block(J, group)
        rcopy(ref, ref, ss.at[J, 0], rr.at[J, slot], partner).wait_recv()

    g_dn, g_up, g_far = pc.group(3, 0), pc.group(1, 0), pc.group(2, 0)

    def own(J):
        for copy in own_copies(J):
            copy.start()

    def stage_a(J):
        arrived(J, 2, g_dn)
        forward(J, g_dn, 3, 4, partner).start()

        @pl.when(J % 2 == 0)
        def _():
            forward(J, g_dn, 6, 6, up).start()

        arrived(J, 3, g_up)
        forward(J, g_up, 4, 5, partner).start()

        @pl.when(J % 2 == 1)
        def _():
            forward(J, g_up, 6, 6, down).start()

    def stage_b(J):
        @pl.when(J % 2 == 0)
        def _():
            arrived(J, 5, pc.group(1, 1))
            forward(J, pc.group(1, 1), 5, 7, down).start()

        @pl.when(J % 2 == 1)
        def _():
            arrived(J, 4, pc.group(3, 1))
            forward(J, pc.group(3, 1), 5, 7, up).start()

    def stage_c(J):
        @pl.when(J % 2 == 0)
        def _():
            arrived(J, 4, pc.group(3, 1))

        @pl.when(J % 2 == 1)
        def _():
            arrived(J, 5, pc.group(1, 1))

        arrived(J, 1, pc.group(0, 1))
        arrived(J, 6, g_far)
        arrived(J, 7, pc.group(2, 1))
        h, cols = part(J)
        even = h % 2
        x = xall[h, :, :, cols].reshape(NR, KCH)

        @pl.when(J % NCH == 0)
        def _():
            acc[even] = jnp.zeros(acc.shape[1:], F32)
            accm[even] = jnp.zeros(accm.shape[1:], F32)

        accm[even] += lax.dot_general(
            dn[:, cols], x, (((1,), (1,)), ((), ())), preferred_element_type=F32
        )
        acc[even] += jnp.dot(x, w[cols, :], preferred_element_type=F32)

    def table_copies(k, dy, flip):
        device = pc.peer(dy, flip)
        i = pc.group(dy, flip)
        qc = pl.ds(pl.multiple_of(i * QC, QC), QC)
        kc = pl.ds(pl.multiple_of(i * KVC, KVC), KVC)
        return (
            rcopy(uq.at[:, qc], uq_all.at[pc.g], ts.at[k, 0], tr.at[k, 0], device),
            rcopy(ukv.at[0, :, kc], uk_all.at[pc.g], ts.at[k, 1], tr.at[k, 1], device),
            rcopy(ukv.at[1, :, kc], uv_all.at[pc.g], ts.at[k, 2], tr.at[k, 2], device),
        )

    def late_copies():
        copies = [rcopy(uo_hbm, uo.at[pc.xl], ts.at[0, 4], tr.at[0, 4], partner)]
        for k, (dy, flip) in enumerate(PEERS):
            i = pc.group(dy, flip)
            qc = pl.ds(pl.multiple_of(i * QC, QC), QC)
            copies.append(
                rcopy(do.at[:, qc], do_all.at[pc.g], ts.at[k, 3], tr.at[k, 3], pc.peer(dy, flip))
            )
        return copies

    sub = lax.broadcasted_iota(jnp.int32, (HR, HD), 0)
    low = lax.broadcasted_iota(jnp.int32, (HR, HD), 1) < HD // 2

    def rotation(h, b):
        pos = 64 * (z * 4 + pc.quarter(b)) + HR * h + sub
        begin = jnp.zeros((HR, HD), jnp.int32)
        end = jnp.int32(0)
        for r in range(REQS):
            length = lens[b, r]
            end = end + length
            begin = begin + jnp.where(pos >= end, length, 0)
        angle = (pos - begin).astype(F32) * freq[...]
        rows = pl.ds(pl.multiple_of(h * NR + b * HR, HR), HR)
        cosb[rows, :] = jnp.cos(angle)
        sine = jnp.sin(angle)
        sinb[rows, :] = jnp.where(low, -sine, sine)

    def mid_copies(h):
        return [
            rcopy(midsend.at[h], mid_all.at[h, pc.g], ms.at[h, k], mr.at[h, k], pc.peer(*p))
            for k, p in enumerate(PEERS)
        ]

    def finish_mid(h):
        keep = (row_slots(pc, range(8), HR, HR * h, lens, adap, aslot) == pc.g).astype(F32)
        mid = (accm[h % 2] * keep).astype(BF16).reshape(3, RK, NR)
        midsend[h] = mid
        mid_all[h, pc.g] = mid
        for copy in mid_copies(h):
            copy.start()

    def kv_row(zsrc, quarter, h):
        return (zsrc * 4 + quarter) * H + h

    def z_copies(h, d):
        zd = (z + d) % 8
        device = pc.level(zd)
        return (
            rcopy(kvbuf.at[h, zd], kv_all.at[kv_row(z, pc.quarter(zd), h)], zs_s.at[h, d, 1], zs_r.at[h, d, 1], device),
            rcopy(qbuf.at[h, zd], q_all.at[z, h], zs_s.at[h, d, 0], zs_r.at[h, d, 0], device),
        )

    def finish_rows(h):
        for copy in mid_copies(h):
            copy.wait_recv()
        even = h % 2
        rows = pl.ds(pl.multiple_of(h * NR, NR), NR)
        cosv, sinv = cosb[rows, :], sinb[rows, :]

        def widen(which, table, base):
            mid = mid_all[h, :, which].reshape(8 * RK, NR)
            delta = lax.dot_general(
                mid, table[...].reshape(8 * RK, table.shape[2]), (((0,), (0,)), ((), ())),
                preferred_element_type=F32,
            )
            return base + 2.0 * delta

        def rope(v):
            return v * cosv + pltpu.roll(v, HD // 2, 1) * sinv

        key = rope(widen(1, uk_all, acc[even, :, QC : QC + KVC]))
        kvbuf[h, :, :, 0:HD] = key.astype(BF16).reshape(8, HR, HD)
        value = widen(2, uv_all, acc[even, :, QC + KVC : QC + 2 * KVC])
        kvbuf[h, :, :, HD : 2 * HD] = value.astype(BF16).reshape(8, HR, HD)
        kv_all[kv_row(z, q_own, h)] = kvbuf[h, z]
        for d in (4, 3, 5, 2, 6, 1, 7):
            z_copies(h, d)[0].start()
        query = widen(0, uq_all, acc[even, :, 0:QC])
        for j in range(4):
            qbuf[h, :, :, j * HD : (j + 1) * HD] = (
                rope(query[:, j * HD : (j + 1) * HD]).astype(BF16).reshape(8, HR, HD)
            )
        q_all[z, h] = qbuf[h, z]
        for d in (4, 3, 5, 2, 6, 1, 7):
            z_copies(h, d)[1].start()

    q_own = pc.quarter(z)
    q_across = (1 - q_own // 2) * 2 + pc.co
    xh_mate = jnp.where((z % 2) == pc.xl, pc.xh, (pc.xh + 1 - pc.co) % 2)
    q_mate = xh_mate * 2 + 1 - pc.co
    q_mate_across = (1 - xh_mate) * 2 + 1 - pc.co

    def kv_copy(quarter, h, d, k, device):
        ref = kv_all.at[kv_row((z + 8 - d) % 8, quarter, h)]
        return rcopy(ref, ref, gs.at[h, k, d], gr.at[h, k, d], device)

    def spread_own(h):
        def one(d, carry):
            @pl.when(d > 0)
            def _():
                z_copies(h, d)[0].wait_recv()

            kv_copy(q_own, h, d, 1, across).start()
            kv_copy(q_own, h, d, 0, mate).start()
            return carry

        lax.fori_loop(0, 8, one, None)

    def spread_across(h):
        def one(d, carry):
            kv_copy(q_across, h, d, 1, across).wait_recv()
            kv_copy(q_across, h, d, 2, mate).start()
            return carry

        lax.fori_loop(0, 8, one, None)

    def due(t, lag, run):
        last = t - lag

        @pl.when((last >= 0) & (last < NJ) & (last % NCH == NCH - 1))
        def _():
            run(last // NCH)

    def step(t, carry=None):
        @pl.when(t + LEAD < NJ)
        def _():
            own(t + LEAD)

        @pl.when(t < NJ)
        def _():
            stage_a(t)

        @pl.when((t >= LAG_B) & (t < NJ + LAG_B))
        def _():
            stage_b(t - LAG_B)

        @pl.when(t < NJ)
        def _():
            for i in range(8 // NCH):
                rotation(t // NCH, (t % NCH) * (8 // NCH) + i)

        @pl.when(t == LAG_C)
        def _():
            for k, p in enumerate(PEERS):
                for copy in table_copies(k, *p):
                    copy.wait_recv()

        @pl.when((t >= LAG_C) & (t < NJ + LAG_C))
        def _():
            stage_c(t - LAG_C)

        due(t, LAG_C, finish_mid)
        due(t, LAG_ROWS, finish_rows)
        due(t, LAG_OWN, spread_own)
        due(t, LAG_ACROSS, spread_across)
        return carry

    for J in range(LEAD):
        own(J)
    for k, p in enumerate(PEERS):
        for copy in table_copies(k, *p):
            copy.start()
    for load in loads:
        load.wait()
    lax.fori_loop(0, NJ + LAG_ACROSS, step, None)
    for copy in late_copies():
        copy.start()

    def collect(i, carry):
        h, d = i // 8, i % 8
        kv_copy(q_mate, h, d, 0, mate).wait_recv()
        kv_copy(q_mate_across, h, d, 2, mate).wait_recv()

        @pl.when(d > 0)
        def _():
            z_copies(h, d)[1].wait_recv()

        return carry

    lax.fori_loop(0, H * 8, collect, None)

    col = lax.broadcasted_iota(jnp.int32, (4 * BR, CK), 1)
    row1 = lax.broadcasted_iota(jnp.int32, (4 * BR, 1), 0) % BR
    scale = math.log2(math.e) / math.sqrt(HD)
    bk = CK // HR

    def offset_of(k):
        return 4 + jnp.where(k % 2 == 0, k // 2, -((k + 1) // 2))

    def back_copy(half, k):
        zd = (z + offset_of(k)) % 8
        return rcopy(att_buf.at[half, zd], att_all.at[half, z // 2, z % 2], as_.at[half, k], ar.at[half, k], pc.level(zd))

    def attend(it, carry):
        half, k = it // 8, it % 8
        zq = (z + offset_of(k)) % 8
        first = 64 * (zq * 4 + q_own) + BR * half
        pos = first + row1
        begin = jnp.zeros((4 * BR, 1), jnp.int32)
        end = jnp.int32(0)
        for r in range(REQS):
            length = lens[z, r]
            end = end + length
            begin = begin + jnp.where(pos >= end, length, 0)
        q = q_all[zq, pl.ds(half * (BR // HR), BR // HR)].reshape(BR, QC)
        q = jnp.concatenate([q[:, j * HD : (j + 1) * HD] for j in range(4)], axis=0)

        start = jnp.maximum(first + BR - NK * CK, 0)
        scores = []
        for i in range(NK):
            keys = kv_all[pl.ds(start // HR + i * bk, bk), :, 0:HD].reshape(CK, HD)
            s = lax.dot_general(q, keys, (((1,), (1,)), ((), ())), preferred_element_type=F32) * scale
            at = col + (start + i * CK)
            scores.append(jnp.where((at >= begin) & (at <= pos), s, NEG))
        top = functools.reduce(jnp.maximum, [jnp.max(s, axis=1, keepdims=True) for s in scores])
        total = jnp.zeros((4 * BR, 1), F32)
        accum = jnp.zeros((4 * BR, HD), F32)
        for i, s in enumerate(scores):
            values = kv_all[pl.ds(start // HR + i * bk, bk), :, HD : 2 * HD].reshape(CK, HD)
            p = jnp.exp2(s - top)
            total += jnp.sum(p, axis=1, keepdims=True)
            accum += jnp.dot(p.astype(BF16), values, preferred_element_type=F32)
        result = (accum / total).astype(BF16)
        for j in range(4):
            att_buf[half, zq, :, j * HD : (j + 1) * HD] = result[j * BR : (j + 1) * BR]

        @pl.when(k < 7)
        def _():
            back_copy(half, k).start()

        @pl.when(k == 7)
        def _():
            att_all[half, z // 2, z % 2] = att_buf[half, z]

        return carry

    def om_copy(half, k, dy, flip):
        to = pc.group(dy, flip)
        return rcopy(
            omsend.at[half, to % 2, to // 2], om_recv.at[half, pc.g], os_.at[half, k], or_.at[half, k],
            pc.peer(dy, flip),
        )

    def mid_send(half):
        for column in range(2):
            rows = att_all[half, :, column].reshape(4 * BR, QC)
            omsend[half, column] = lax.dot_general(
                do_all[...].reshape(8 * RK, QC), rows, (((1,), (1,)), ((), ())), preferred_element_type=F32
            ).reshape(4, 2 * RK, 4 * BR)
        for k, p in enumerate(PEERS):
            om_copy(half, k, *p).start()
        om_recv[half, pc.g] = omsend[half, pc.xl, pc.y]

    def mid_done(half):
        groups = [b * 2 + pc.xl for b in range(4)]
        slots = row_slots(pc, groups, BR, BR * half, lens, adap, aslot)
        mine = 2 * pc.y + lax.broadcasted_iota(jnp.int32, (2 * RK, 4 * BR), 0) // RK
        keep = (slots == mine).astype(F32)
        for k, p in enumerate(PEERS):
            om_copy(half, k, *p).wait_recv()
        om[half] = (jnp.sum(om_recv[half], axis=0) * keep).astype(BF16)

    def att_ready(half):
        for k in range(7):
            back_copy(half, k).wait_recv()

    y_far, y_up, y_dn = (pc.y + 2) % 4, (pc.y + 1) % 4, (pc.y + 3) % 4

    def x_copy(J):
        return rcopy(pbuf.at[J, :, 1 - pc.xl], xrecv.at[J], xs.at[J], xr.at[J], partner)

    def far_copy(J, odd):
        return rcopy(sbuf.at[J, y_far], far.at[J], ys.at[J, 0], yr.at[J, 0], down if odd else up)

    def up_copy(J):
        return rcopy(tup.at[J], rup.at[J], ys.at[J, 1], yr.at[J, 1], up)

    def dn_copy(J):
        return rcopy(tdn.at[J], rdn.at[J], ys.at[J, 2], yr.at[J, 2], down)

    def stage_p(J):
        half = J // NN
        cols = pl.ds(pl.multiple_of((J % NN) * NC, NC), NC)
        rows = att_all[half].reshape(8 * BR, QC)
        total = jnp.dot(rows, wo[:, cols], preferred_element_type=F32)
        pbuf[J] = total.astype(BF16).reshape(4, 2, BR, NC)
        x_copy(J).start()

    def stage_s(J, odd):
        half = J // NN
        cols = pl.ds(pl.multiple_of((J % NN) * NC, NC), NC)
        delta = lax.dot_general(
            om[half], uo[:, :, cols].reshape(2 * RK, NC), (((0,), (0,)), ((), ())), preferred_element_type=F32
        ).reshape(4, BR, NC)
        x_copy(J).wait_recv()
        total = pbuf[J, :, pc.xl].astype(F32) + xrecv[J].astype(F32) + 2.0 * delta
        sbuf[J] = total.astype(BF16)
        far_copy(J, odd).start()
        if odd:
            tup[J] = sbuf[J, y_up]
            up_copy(J).start()
        else:
            tdn[J] = sbuf[J, y_dn]
            dn_copy(J).start()

    def stage_t(J, odd):
        far_copy(J, odd).wait_recv()
        if odd:
            tdn[J] = (sbuf[J, y_dn].astype(F32) + far[J].astype(F32)).astype(BF16)
            dn_copy(J).start()
        else:
            tup[J] = (sbuf[J, y_up].astype(F32) + far[J].astype(F32)).astype(BF16)
            up_copy(J).start()

    def stage_f(J):
        up_copy(J).wait_recv()
        dn_copy(J).wait_recv()
        half = J // NN
        cols = pl.ds(pl.multiple_of((J % NN) * NC, NC), NC)
        total = sbuf[J, pc.y].astype(F32) + rup[J].astype(F32) + rdn[J].astype(F32)
        out[pl.ds(pl.multiple_of(half * BR, BR), BR), cols] = total

    def turn(t, carry=None):
        @pl.when((t >= 1) & (t < NT // 2 + 1))
        def _():
            stage_s(2 * t - 2, False)
            stage_s(2 * t - 1, True)

        @pl.when((t >= 2) & (t < NT // 2 + 2))
        def _():
            stage_t(2 * t - 4, False)
            stage_t(2 * t - 3, True)

        @pl.when(t >= 3)
        def _():
            stage_f(2 * t - 6)
            stage_f(2 * t - 5)

        return carry

    lax.fori_loop(0, 16, attend, None)
    for copy in late_copies():
        copy.wait_recv()
    att_ready(0)
    mid_send(0)

    def whole(t, carry):
        @pl.when(t < NT // 2)
        def _():
            stage_p(2 * t)
            stage_p(2 * t + 1)

        @pl.when(t == 0)
        def _():
            mid_done(0)

        @pl.when(t == NN // 2 - 2)
        def _():
            att_ready(1)
            mid_send(1)

        @pl.when(t == NN // 2)
        def _():
            mid_done(1)

        return turn(t, carry)

    lax.fori_loop(0, NT // 2 + 3, whole, None)

    def drain_z(i, carry):
        h, d = i // 8, i % 8

        @pl.when(d > 0)
        def _():
            kv, q = z_copies(h, d)
            kv.wait_send()
            q.wait_send()

        kv_copy(q_own, h, d, 1, across).wait_send()
        kv_copy(q_own, h, d, 0, mate).wait_send()
        kv_copy(q_across, h, d, 2, mate).wait_send()
        return carry

    lax.fori_loop(0, H * 8, drain_z, None)

    def drain_mid(h, carry):
        for copy in mid_copies(h):
            copy.wait_send()
        return carry

    lax.fori_loop(0, H, drain_mid, None)

    def drain_back(half, carry):
        for k in range(7):
            back_copy(half, k).wait_send()
        for k, p in enumerate(PEERS):
            om_copy(half, k, *p).wait_send()
        return carry

    lax.fori_loop(0, 2, drain_back, None)
    for k, p in enumerate(PEERS):
        for copy in table_copies(k, *p):
            copy.wait_send()
    for copy in late_copies():
        copy.wait_send()

    def drain_tok(J, carry):
        for copy in own_copies(J):
            copy.wait_send()
        for k in range(3, 7):
            forward(J, pc.g, k, 0, partner).wait_send()
        return carry

    lax.fori_loop(0, NJ, drain_tok, None)

    def drain_out(J, carry):
        x_copy(J).wait_send()
        far_copy(J, False).wait_send()
        up_copy(J).wait_send()
        dn_copy(J).wait_send()
        return carry

    lax.fori_loop(0, NT, drain_out, None)


def layer(*args):
    any_ = pl.BlockSpec(memory_space=pl.ANY)
    vmem = pl.BlockSpec(memory_space=pltpu.VMEM)
    smem = pl.BlockSpec(memory_space=pltpu.SMEM)
    dma = pltpu.SemaphoreType.DMA
    return pl.pallas_call(
        layer_kernel,
        name="layer",
        out_shape=jax.ShapeDtypeStruct((64, D), F32),
        in_specs=[smem] * 3 + [any_] * 10 + [vmem],
        out_specs=vmem,
        scratch_shapes=[
            pltpu.VMEM((H, 8, HR, D), BF16),
            pltpu.VMEM((D, QC + 2 * KVC), BF16),
            pltpu.VMEM((QC, D), BF16),
            pltpu.VMEM((3 * RK, D), BF16),
            pltpu.VMEM((2, RK, D), BF16),
            pltpu.VMEM((2, NR, QC + 2 * KVC), F32),
            pltpu.VMEM((2, 3 * RK, NR), F32),
            pltpu.VMEM((8, RK, QC), BF16),
            pltpu.VMEM((8, RK, KVC), BF16),
            pltpu.VMEM((8, RK, KVC), BF16),
            pltpu.VMEM((8, RK, QC), BF16),
            pltpu.VMEM((H, 3, RK, NR), BF16),
            pltpu.VMEM((H, 8, 3, RK, NR), BF16),
            pltpu.VMEM((H, 8, HR, QC), BF16),
            pltpu.VMEM((H, 8, HR, 2 * HD), BF16),
            pltpu.VMEM((512, HD), F32),
            pltpu.VMEM((512, HD), F32),
            pltpu.VMEM((8, H, HR, QC), BF16),
            pltpu.VMEM((32 * H, HR, 2 * HD), BF16),
            pltpu.VMEM((2, 8, BR, QC), BF16),
            pltpu.VMEM((2, 4, 2, BR, QC), BF16),
            pltpu.VMEM((2, 2, 4, 2 * RK, 4 * BR), F32),
            pltpu.VMEM((2, 8, 2 * RK, 4 * BR), F32),
            pltpu.VMEM((2, 2 * RK, 4 * BR), BF16),
            pltpu.VMEM((NT, 4, 2, BR, NC), BF16),
            pltpu.VMEM((NT, 4, BR, NC), BF16),
            pltpu.VMEM((NT, 4, BR, NC), BF16),
            pltpu.VMEM((NT, BR, NC), BF16),
            pltpu.VMEM((NT, BR, NC), BF16),
            pltpu.VMEM((NT, BR, NC), BF16),
            pltpu.VMEM((NT, BR, NC), BF16),
            pltpu.VMEM((NT, BR, NC), BF16),
            dma((10 + H,)),
            dma((7, 5)),
            dma((7, 5)),
            dma((NJ, 7)),
            dma((NJ, 8)),
            dma((H, 7)),
            dma((H, 7)),
            dma((H, 8, 2)),
            dma((H, 8, 2)),
            dma((H, 3, 8)),
            dma((H, 3, 8)),
            dma((2, 8)),
            dma((2, 8)),
            dma((2, 7)),
            dma((2, 7)),
            dma((NT,)),
            dma((NT,)),
            dma((NT, 3)),
            dma((NT, 3)),
        ],
        compiler_params=pltpu.CompilerParams(
            collective_id=0, has_side_effects=True, vmem_limit_bytes=61 << 20
        ),
    )(*args)


def body(
    tokens, req_lengths, req_adapter, adapter_slot, query_weight, key_weight, value_weight, w_out,
    down_qkv, up_query, up_kv, down_out, up_out,
):
    half = np.arange(HD) % (HD // 2)
    freq = jnp.asarray(np.exp(half * (-2.0 * math.log(ROPE_BASE) / HD)).astype(np.float32)[None, :])
    out = layer(
        req_lengths, req_adapter, adapter_slot, tokens[0], query_weight, key_weight, value_weight, w_out,
        down_qkv[0], up_query[0], up_kv[0], down_out[0], up_out[0], freq,
    )
    return out.astype(BF16)[None]


def solution(mesh):
    placed = (
        P("grp", "ctx", None),
        P(),
        P(),
        P(),
        P(None, "grp"),
        P(None, "grp"),
        P(None, "grp"),
        P("grp", None),
        P("grp", None, None),
        P("grp", None, None),
        P("grp", None, None, None),
        P("grp", None, None),
        P("grp", None, None),
    )
    return jax.shard_map(
        body, mesh=mesh, in_specs=placed, out_specs=P("grp", "ctx", None), check_vma=False
    )
```

time: 639 us -> 121 us (0.19)
  waiting for transfers between devices: 512 us -> 0 us
  Pallas kernels: 0 us -> 118 us
  matrix products: 49.3 us -> 0 us
  blocking collectives: 33 us -> 0 us
  other arithmetic: 16.3 us -> 2.07 us
  between operations: 13.5 us -> 0.01 us
  local copies, waits for them, and re-layouts: 13 us -> 0 us
    all_gather x7 -> x0, waiting for transfers between devices: 372 us -> none  [the longest x1 91.5 us: body(): all_requests = lax.all_gather(tokens, 'grp', axis=0, tiled=True)]
    reduce_scatter x2 -> x0, waiting for transfers between devices: 136 us -> none  [the longest x1 96.8 us: body(): lax.psum_scatter(lax.optimization_barrier(partial_term.astype(jnp.bfloat1...]
    pallas_call x0 -> x1, Pallas kernels: none -> 118 us  [layer(): pl.pallas_call(layer_kernel, name='layer', out_shape=jax.ShapeDtypeStruct...]
    dot_general x12 -> x0, matrix products: 49.3 us -> none  [the longest x1 9.97 us: body(): jnp.einsum('gtkjd,gskd->gtkjs', query, key_heads, preferred_element_type=...]
    all_gather x1 -> x0, blocking collectives: 33 us -> none  [body(): lax.all_gather(up_kv, 'grp', axis=0, tiled=True)]
    reduce_sum x4 -> x0, other arithmetic: 9.69 us -> none  [the longest x1 8.58 us: body(): new_sum = jnp.sum(weights, axis=-1)]
    gather x5 -> x0, local copies, waits for them, and re-layouts: 7.85 us -> none  [the longest x1 4.34 us: body(): down_adapter = jnp.take(down_slots, adapter_slot, axis=0)]
  transfers between devices with their start and end apart: 9 -> 0, of which waited for: 9 -> 0; matrix products, arithmetic and copies ran while one was open for 12% -> 0% of each run, Pallas kernels for 0% -> 0%
where the time goes in v2:
time: 121 us; the launch traced here: 120 us
  Pallas kernels  118 us (98%)
  other arithmetic  2.07 us (2%)
    pallas_call x1, Pallas kernels, layer(): pl.pallas_call(layer_kernel, name='layer', out_shape=jax.ShapeDtypeStruct...  118 us

profile of v2, /device:TPU:2, one launch (start us, length us, event | category | flops | bytes accessed | tf_op | source)
XLA Modules:
  0.0 120.2 jit_solution(7582685326828454638)
XLA Ops:
  0.0 118.1 %layer.1 = f32[64,4096]{1,0:T(8,128)} custom-call(s32[8,8]{1,0:T(8,128)} %lens.1, s32[8,8]{1,0:T(8,128)} %adap.1, s32[8]{0:T(128)} %aslot.1, bf16[64,4096]{1,0:T(8,128)(2,1)} %bitcast.8, bf16[4096,512]{1,0:T(8,128)(2,1)} %wq.1, bf16[4096,128]{1,0:T(8,128)(2,1)} %wk.1, bf16[4096,128]{1,0:T(8,128)(2,1)} %wv.1, bf16[512,4096]{1,0:T(8,128)(2,1)} %w_out.1, ...), custom_call_target="tpu_custom_call" | custom-call | tf_op jit(solution)/shard_map/layer/pallas_call | solution.py:661
  118.1 2.1 %convert_bitcast_fusion = bf16[1,64,4096]{2,1,0:T(8,128)(2,1)} fusion(f32[64,4096]{1,0:T(8,128)} %layer.1), kind=kLoop, calls=%fused_computation | loop fusion | flops 262144 | bytes 1572864 | tf_op jit(solution)/shard_map/broadcast_in_dim | solution.py:736

commit v3 on v2

--- a/solution.py
+++ b/solution.py
@@ -24,17 +24,18 @@
 H = 4
 HR = 64 // H
 NR = 8 * HR
-NCH = 4
+NCH = 2
 KCH = D // NCH
 NJ = H * NCH
-LEAD = 5
-LAG_B, LAG_C, LAG_ROWS, LAG_OWN, LAG_ACROSS = 2, 5, 7, 11, 13
+LEAD = 4
+LAG_B, LAG_C, LAG_ROWS, LAG_OWN, LAG_ACROSS = 2, 5, 5+2, 5+4, 5+5
 BR = 32
 CK = 384
 NK = -(-(1088 + BR - 1) // CK)
 NC = 512
 NN = D // NC
 NT = 2 * NN
+READY = 11
 
 
 class Place:
@@ -70,6 +71,10 @@
     return pltpu.make_async_remote_copy(
         src_ref=src, dst_ref=dst, send_sem=ssem, recv_sem=rsem, device_id=device, device_id_type=MESH
     )
+
+
+def take(ref, sem):
+    pltpu.make_async_copy(ref, ref, sem).wait()
 
 
 def greet(devices):
@@ -99,7 +104,7 @@
     out,
     xall, w, wo, dn, uo, acc, accm, uq_all, uk_all, uv_all, do_all, midsend, mid_all, qbuf, kvbuf,
     cosb, sinb, q_all, kv_all, att_buf, att_all, omsend, om_recv, om, pbuf, xrecv, sbuf, far, tup, tdn, rup, rdn,
-    lsem, ts, tr, ss, rr, ms, mr, zs_s, zs_r, gs, gr, as_, ar, os_, or_, xs, xr, ys, yr,
+    lsem, sent, tr, rr, mr, zr, gr, ar, orr, xr, yr,
 ):
     pc = Place()
     z = pc.z
@@ -111,7 +116,7 @@
     qcols = pl.ds(pl.multiple_of(pc.g * QC, QC), QC)
     kcols = pl.ds(pl.multiple_of(pc.g * KVC, KVC), KVC)
 
-    local = [
+    local = [(tok.at[h * HR : (h + 1) * HR, :], xall.at[h, pc.g]) for h in range(H)] + [
         (wq, w.at[:, 0:QC]),
         (wk, w.at[:, QC : QC + KVC]),
         (wv, w.at[:, QC + KVC : QC + 2 * KVC]),
@@ -120,7 +125,6 @@
         (ukv.at[0, :, kcols], uk_all.at[pc.g]),
         (ukv.at[1, :, kcols], uv_all.at[pc.g]),
         (do.at[:, qcols], do_all.at[pc.g]),
-    ] + [(tok.at[h * HR : (h + 1) * HR, :], xall.at[h, pc.g]) for h in range(H)] + [
         (uo_hbm, uo.at[pc.xl]),
         (w_out, wo),
     ]
@@ -142,67 +146,64 @@
         return xall.at[h, group, :, cols]
 
     def own_copies(J):
+        src = dst = block(J, pc.g)
+        return (
+            rcopy(src, dst, sent.at[0], rr.at[J, 0], up),
+            rcopy(src, dst, sent.at[0], rr.at[J, 1], down),
+            rcopy(src, dst, sent.at[0], rr.at[J, 3], partner),
+        )
+
+    def forward(J, group, wave, device):
+        ref = block(J, group)
+        return rcopy(ref, ref, sent.at[0], rr.at[J, wave], device)
+
+    def arrived(J, wave, blocks=1):
         h, cols = part(J)
-        src = tok.at[pl.ds(pl.multiple_of(h * HR, HR), HR), cols]
-        dst = block(J, pc.g)
-        return (
-            rcopy(src, dst, ss.at[J, 0], rr.at[J, 2], up),
-            rcopy(src, dst, ss.at[J, 1], rr.at[J, 3], down),
-            rcopy(src, dst, ss.at[J, 2], rr.at[J, 1], partner),
-        )
-
-    def forward(J, group, ssem, rslot, device):
-        ref = block(J, group)
-        return rcopy(ref, ref, ss.at[J, ssem], rr.at[J, rslot], device)
-
-    def arrived(J, slot, group):
-        ref = block(J, group)
-        rcopy(ref, ref, ss.at[J, 0], rr.at[J, slot], partner).wait_recv()
-
-    g_dn, g_up, g_far = pc.group(3, 0), pc.group(1, 0), pc.group(2, 0)
+        take(xall.at[h, 0:blocks, :, cols], rr.at[J, wave])
+
+    g_dn, g_up = pc.group(3, 0), pc.group(1, 0)
 
     def own(J):
         for copy in own_copies(J):
             copy.start()
 
     def stage_a(J):
-        arrived(J, 2, g_dn)
-        forward(J, g_dn, 3, 4, partner).start()
+        even = J % 2 == 0
+        arrived(J, 0)
+
+        @pl.when(even)
+        def _():
+            forward(J, g_dn, 3, partner).start()
+            forward(J, g_dn, 3, up).start()
+
+        @pl.when(J % 2 == 1)
+        def _():
+            forward(J, g_dn, 2, partner).start()
+
+        arrived(J, 1)
+
+        @pl.when(even)
+        def _():
+            forward(J, g_up, 2, partner).start()
+
+        @pl.when(J % 2 == 1)
+        def _():
+            forward(J, g_up, 3, partner).start()
+            forward(J, g_up, 3, down).start()
+
+    def stage_b(J):
+        arrived(J, 2)
 
         @pl.when(J % 2 == 0)
         def _():
-            forward(J, g_dn, 6, 6, up).start()
-
-        arrived(J, 3, g_up)
-        forward(J, g_up, 4, 5, partner).start()
+            forward(J, pc.group(1, 1), 3, down).start()
 
         @pl.when(J % 2 == 1)
         def _():
-            forward(J, g_up, 6, 6, down).start()
-
-    def stage_b(J):
-        @pl.when(J % 2 == 0)
-        def _():
-            arrived(J, 5, pc.group(1, 1))
-            forward(J, pc.group(1, 1), 5, 7, down).start()
-
-        @pl.when(J % 2 == 1)
-        def _():
-            arrived(J, 4, pc.group(3, 1))
-            forward(J, pc.group(3, 1), 5, 7, up).start()
+            forward(J, pc.group(3, 1), 3, up).start()
 
     def stage_c(J):
-        @pl.when(J % 2 == 0)
-        def _():
-            arrived(J, 4, pc.group(3, 1))
-
-        @pl.when(J % 2 == 1)
-        def _():
-            arrived(J, 5, pc.group(1, 1))
-
-        arrived(J, 1, pc.group(0, 1))
-        arrived(J, 6, g_far)
-        arrived(J, 7, pc.group(2, 1))
+        arrived(J, 3, 4)
         h, cols = part(J)
         even = h % 2
         x = xall[h, :, :, cols].reshape(NR, KCH)
@@ -223,18 +224,18 @@
         qc = pl.ds(pl.multiple_of(i * QC, QC), QC)
         kc = pl.ds(pl.multiple_of(i * KVC, KVC), KVC)
         return (
-            rcopy(uq.at[:, qc], uq_all.at[pc.g], ts.at[k, 0], tr.at[k, 0], device),
-            rcopy(ukv.at[0, :, kc], uk_all.at[pc.g], ts.at[k, 1], tr.at[k, 1], device),
-            rcopy(ukv.at[1, :, kc], uv_all.at[pc.g], ts.at[k, 2], tr.at[k, 2], device),
+            rcopy(uq.at[:, qc], uq_all.at[pc.g], sent.at[1], tr.at[0], device),
+            rcopy(ukv.at[0, :, kc], uk_all.at[pc.g], sent.at[2], tr.at[1], device),
+            rcopy(ukv.at[1, :, kc], uv_all.at[pc.g], sent.at[3], tr.at[2], device),
         )
 
     def late_copies():
-        copies = [rcopy(uo_hbm, uo.at[pc.xl], ts.at[0, 4], tr.at[0, 4], partner)]
+        copies = [rcopy(uo_hbm, uo.at[pc.xl], sent.at[5], tr.at[4], partner)]
         for k, (dy, flip) in enumerate(PEERS):
             i = pc.group(dy, flip)
             qc = pl.ds(pl.multiple_of(i * QC, QC), QC)
             copies.append(
-                rcopy(do.at[:, qc], do_all.at[pc.g], ts.at[k, 3], tr.at[k, 3], pc.peer(dy, flip))
+                rcopy(do.at[:, qc], do_all.at[pc.g], sent.at[4], tr.at[3], pc.peer(dy, flip))
             )
         return copies
 
@@ -257,7 +258,7 @@
 
     def mid_copies(h):
         return [
-            rcopy(midsend.at[h], mid_all.at[h, pc.g], ms.at[h, k], mr.at[h, k], pc.peer(*p))
+            rcopy(midsend.at[h], mid_all.at[h, pc.g], sent.at[6], mr.at[h], pc.peer(*p))
             for k, p in enumerate(PEERS)
         ]
 
@@ -276,13 +277,12 @@
         zd = (z + d) % 8
         device = pc.level(zd)
         return (
-            rcopy(kvbuf.at[h, zd], kv_all.at[kv_row(z, pc.quarter(zd), h)], zs_s.at[h, d, 1], zs_r.at[h, d, 1], device),
-            rcopy(qbuf.at[h, zd], q_all.at[z, h], zs_s.at[h, d, 0], zs_r.at[h, d, 0], device),
+            rcopy(kvbuf.at[h, zd], kv_all.at[kv_row(z, pc.quarter(zd), h)], sent.at[7], zr.at[h], device),
+            rcopy(qbuf.at[h, zd], q_all.at[z, h], sent.at[8], zr.at[H], device),
         )
 
     def finish_rows(h):
-        for copy in mid_copies(h):
-            copy.wait_recv()
+        take(mid_all.at[h, 0:7], mr.at[h])
         even = h % 2
         rows = pl.ds(pl.multiple_of(h * NR, NR), NR)
         cosv, sinv = cosb[rows, :], sinb[rows, :]
@@ -322,14 +322,12 @@
 
     def kv_copy(quarter, h, d, k, device):
         ref = kv_all.at[kv_row((z + 8 - d) % 8, quarter, h)]
-        return rcopy(ref, ref, gs.at[h, k, d], gr.at[h, k, d], device)
+        return rcopy(ref, ref, sent.at[9], gr.at[jnp.where(k == 1, h, H + k // 2)], device)
 
     def spread_own(h):
+        take(kv_all.at[0:7], zr.at[h])
+
         def one(d, carry):
-            @pl.when(d > 0)
-            def _():
-                z_copies(h, d)[0].wait_recv()
-
             kv_copy(q_own, h, d, 1, across).start()
             kv_copy(q_own, h, d, 0, mate).start()
             return carry
@@ -337,8 +335,9 @@
         lax.fori_loop(0, 8, one, None)
 
     def spread_across(h):
+        take(kv_all.at[0:8], gr.at[h])
+
         def one(d, carry):
-            kv_copy(q_across, h, d, 1, across).wait_recv()
             kv_copy(q_across, h, d, 2, mate).start()
             return carry
 
@@ -371,9 +370,8 @@
 
         @pl.when(t == LAG_C)
         def _():
-            for k, p in enumerate(PEERS):
-                for copy in table_copies(k, *p):
-                    copy.wait_recv()
+            for i, table in enumerate((uq_all, uk_all, uv_all)):
+                take(table.at[0:7], tr.at[i])
 
         @pl.when((t >= LAG_C) & (t < NJ + LAG_C))
         def _():
@@ -385,29 +383,22 @@
         due(t, LAG_ACROSS, spread_across)
         return carry
 
+    for load in loads[:H]:
+        load.wait()
     for J in range(LEAD):
         own(J)
     for k, p in enumerate(PEERS):
         for copy in table_copies(k, *p):
             copy.start()
-    for load in loads:
+    for load in loads[H:]:
         load.wait()
     lax.fori_loop(0, NJ + LAG_ACROSS, step, None)
     for copy in late_copies():
         copy.start()
 
-    def collect(i, carry):
-        h, d = i // 8, i % 8
-        kv_copy(q_mate, h, d, 0, mate).wait_recv()
-        kv_copy(q_mate_across, h, d, 2, mate).wait_recv()
-
-        @pl.when(d > 0)
-        def _():
-            z_copies(h, d)[1].wait_recv()
-
-        return carry
-
-    lax.fori_loop(0, H * 8, collect, None)
+    take(q_all.at[0:7], zr.at[H])
+    for k in range(2):
+        take(kv_all.at[0 : 8 * H], gr.at[H + k])
 
     col = lax.broadcasted_iota(jnp.int32, (4 * BR, CK), 1)
     row1 = lax.broadcasted_iota(jnp.int32, (4 * BR, 1), 0) % BR
@@ -419,7 +410,7 @@
 
     def back_copy(half, k):
         zd = (z + offset_of(k)) % 8
-        return rcopy(att_buf.at[half, zd], att_all.at[half, z // 2, z % 2], as_.at[half, k], ar.at[half, k], pc.level(zd))
+        return rcopy(att_buf.at[half, zd], att_all.at[half, z // 2, z % 2], sent.at[10], ar.at[half], pc.level(zd))
 
     def attend(it, carry):
         half, k = it // 8, it % 8
@@ -467,7 +458,7 @@
     def om_copy(half, k, dy, flip):
         to = pc.group(dy, flip)
         return rcopy(
-            omsend.at[half, to % 2, to // 2], om_recv.at[half, pc.g], os_.at[half, k], or_.at[half, k],
+            omsend.at[half, to % 2, to // 2], om_recv.at[half, pc.g], sent.at[11], orr.at[half],
             pc.peer(dy, flip),
         )
 
@@ -486,27 +477,25 @@
         slots = row_slots(pc, groups, BR, BR * half, lens, adap, aslot)
         mine = 2 * pc.y + lax.broadcasted_iota(jnp.int32, (2 * RK, 4 * BR), 0) // RK
         keep = (slots == mine).astype(F32)
-        for k, p in enumerate(PEERS):
-            om_copy(half, k, *p).wait_recv()
+        take(om_recv.at[half, 0:7], orr.at[half])
         om[half] = (jnp.sum(om_recv[half], axis=0) * keep).astype(BF16)
 
     def att_ready(half):
-        for k in range(7):
-            back_copy(half, k).wait_recv()
+        take(att_buf.at[half, 0:7], ar.at[half])
 
     y_far, y_up, y_dn = (pc.y + 2) % 4, (pc.y + 1) % 4, (pc.y + 3) % 4
 
     def x_copy(J):
-        return rcopy(pbuf.at[J, :, 1 - pc.xl], xrecv.at[J], xs.at[J], xr.at[J], partner)
+        return rcopy(pbuf.at[J, :, 1 - pc.xl], xrecv.at[J], sent.at[12], xr.at[J // 2], partner)
 
     def far_copy(J, odd):
-        return rcopy(sbuf.at[J, y_far], far.at[J], ys.at[J, 0], yr.at[J, 0], down if odd else up)
+        return rcopy(sbuf.at[J, y_far], far.at[J], sent.at[13], yr.at[J // 2, 0], down if odd else up)
 
     def up_copy(J):
-        return rcopy(tup.at[J], rup.at[J], ys.at[J, 1], yr.at[J, 1], up)
+        return rcopy(tup.at[J], rup.at[J], sent.at[14], yr.at[J // 2, 1], up)
 
     def dn_copy(J):
-        return rcopy(tdn.at[J], rdn.at[J], ys.at[J, 2], yr.at[J, 2], down)
+        return rcopy(tdn.at[J], rdn.at[J], sent.at[15], yr.at[J // 2, 1], down)
 
     def stage_p(J):
         half = J // NN
@@ -522,7 +511,6 @@
         delta = lax.dot_general(
             om[half], uo[:, :, cols].reshape(2 * RK, NC), (((0,), (0,)), ((), ())), preferred_element_type=F32
         ).reshape(4, BR, NC)
-        x_copy(J).wait_recv()
         total = pbuf[J, :, pc.xl].astype(F32) + xrecv[J].astype(F32) + 2.0 * delta
         sbuf[J] = total.astype(BF16)
         far_copy(J, odd).start()
@@ -534,7 +522,6 @@
             dn_copy(J).start()
 
     def stage_t(J, odd):
-        far_copy(J, odd).wait_recv()
         if odd:
             tdn[J] = (sbuf[J, y_dn].astype(F32) + far[J].astype(F32)).astype(BF16)
             dn_copy(J).start()
@@ -543,118 +530,85 @@
             up_copy(J).start()
 
     def stage_f(J):
-        up_copy(J).wait_recv()
-        dn_copy(J).wait_recv()
         half = J // NN
         cols = pl.ds(pl.multiple_of((J % NN) * NC, NC), NC)
         total = sbuf[J, pc.y].astype(F32) + rup[J].astype(F32) + rdn[J].astype(F32)
         out[pl.ds(pl.multiple_of(half * BR, BR), BR), cols] = total
 
-    def turn(t, carry=None):
-        @pl.when((t >= 1) & (t < NT // 2 + 1))
-        def _():
-            stage_s(2 * t - 2, False)
-            stage_s(2 * t - 1, True)
-
-        @pl.when((t >= 2) & (t < NT // 2 + 2))
-        def _():
-            stage_t(2 * t - 4, False)
-            stage_t(2 * t - 3, True)
-
-        @pl.when(t >= 3)
-        def _():
-            stage_f(2 * t - 6)
-            stage_f(2 * t - 5)
+    HP = NN // 2
+
+    def pair_p(u):
+        stage_p(2 * u)
+        stage_p(2 * u + 1)
+
+    def attend_and_project(it, carry):
+        attend(it, carry)
+
+        @pl.when(it == READY)
+        def _():
+            take(do_all.at[0:7], tr.at[3])
+            take(uo.at[0], tr.at[4])
+            att_ready(0)
+            mid_send(0)
+
+        @pl.when((it >= READY) & (it < READY + HP))
+        def _():
+            pair_p(it - READY)
 
         return carry
 
-    lax.fori_loop(0, 16, attend, None)
-    for copy in late_copies():
-        copy.wait_recv()
-    att_ready(0)
-    mid_send(0)
-
-    def whole(t, carry):
-        @pl.when(t < NT // 2)
-        def _():
-            stage_p(2 * t)
-            stage_p(2 * t + 1)
-
-        @pl.when(t == 0)
-        def _():
-            mid_done(0)
-
-        @pl.when(t == NN // 2 - 2)
+    lax.fori_loop(0, 16, attend_and_project, None)
+    mid_done(0)
+
+    def reduce(t, carry):
+        @pl.when(t == HP)
+        def _():
+            mid_done(1)
+
+        @pl.when(t < 2 * HP)
+        def _():
+            take(xrecv.at[0:2], xr.at[t])
+            stage_s(2 * t, False)
+            stage_s(2 * t + 1, True)
+
+        @pl.when((t >= 1) & (t < 2 * HP + 1))
+        def _():
+            take(far.at[0:2], yr.at[t - 1, 0])
+            stage_t(2 * t - 2, False)
+            stage_t(2 * t - 1, True)
+
+        @pl.when(t >= 2)
+        def _():
+            take(rup.at[0:4], yr.at[t - 2, 1])
+            stage_f(2 * t - 4)
+            stage_f(2 * t - 3)
+
+        @pl.when(t == 1)
         def _():
             att_ready(1)
             mid_send(1)
-
-        @pl.when(t == NN // 2)
-        def _():
-            mid_done(1)
-
-        return turn(t, carry)
-
-    lax.fori_loop(0, NT // 2 + 3, whole, None)
-
-    def drain_z(i, carry):
-        h, d = i // 8, i % 8
-
-        @pl.when(d > 0)
-        def _():
-            kv, q = z_copies(h, d)
-            kv.wait_send()
-            q.wait_send()
-
-        kv_copy(q_own, h, d, 1, across).wait_send()
-        kv_copy(q_own, h, d, 0, mate).wait_send()
-        kv_copy(q_across, h, d, 2, mate).wait_send()
+            pair_p(HP)
+
+        @pl.when((t >= 1) & (t < HP))
+        def _():
+            pair_p(t + HP)
+
         return carry
 
-    lax.fori_loop(0, H * 8, drain_z, None)
-
-    def drain_mid(h, carry):
-        for copy in mid_copies(h):
-            copy.wait_send()
-        return carry
-
-    lax.fori_loop(0, H, drain_mid, None)
-
-    def drain_back(half, carry):
-        for k in range(7):
-            back_copy(half, k).wait_send()
-        for k, p in enumerate(PEERS):
-            om_copy(half, k, *p).wait_send()
-        return carry
-
-    lax.fori_loop(0, 2, drain_back, None)
-    for k, p in enumerate(PEERS):
-        for copy in table_copies(k, *p):
-            copy.wait_send()
-    for copy in late_copies():
-        copy.wait_send()
-
-    def drain_tok(J, carry):
-        for copy in own_copies(J):
-            copy.wait_send()
-        for k in range(3, 7):
-            forward(J, pc.g, k, 0, partner).wait_send()
-        return carry
-
-    lax.fori_loop(0, NJ, drain_tok, None)
-
-    def drain_out(J, carry):
-        x_copy(J).wait_send()
-        far_copy(J, False).wait_send()
-        up_copy(J).wait_send()
-        dn_copy(J).wait_send()
-        return carry
-
-    lax.fori_loop(0, NT, drain_out, None)
+    lax.fori_loop(0, 2 * HP + 2, reduce, None)
+
+    for i, ref in enumerate(
+        (
+            xall.at[:, 0:7], uq_all.at[0:7], uk_all.at[0:7], uv_all.at[0:7], do_all.at[0:7], uo.at[0],
+            mid_all.at[:, 0:7], kvbuf.at[:, 0:7], qbuf.at[:, 0:7], kv_all.at[0 : 24 * H],
+            att_buf.at[:, 0:7], om_recv.at[:, 0:7], xrecv, far, rup, rdn,
+        )
+    ):
+        take(ref, sent.at[i])
 
 
 def layer(*args):
-    any_ = pl.BlockSpec(memory_space=pl.ANY)
+    any_ = pl.BlockSpec(memory_space=pltpu.HBM)
     vmem = pl.BlockSpec(memory_space=pltpu.VMEM)
     smem = pl.BlockSpec(memory_space=pltpu.SMEM)
     dma = pltpu.SemaphoreType.DMA
@@ -698,24 +652,16 @@
             pltpu.VMEM((NT, BR, NC), BF16),
             pltpu.VMEM((NT, BR, NC), BF16),
             dma((10 + H,)),
-            dma((7, 5)),
-            dma((7, 5)),
-            dma((NJ, 7)),
-            dma((NJ, 8)),
-            dma((H, 7)),
-            dma((H, 7)),
-            dma((H, 8, 2)),
-            dma((H, 8, 2)),
-            dma((H, 3, 8)),
-            dma((H, 3, 8)),
-            dma((2, 8)),
-            dma((2, 8)),
-            dma((2, 7)),
-            dma((2, 7)),
-            dma((NT,)),
-            dma((NT,)),
-            dma((NT, 3)),
-            dma((NT, 3)),
+            dma((16,)),
+            dma((5,)),
+            dma((NJ, 4)),
+            dma((H,)),
+            dma((H + 1,)),
+            dma((H + 2,)),
+            dma((2,)),
+            dma((2,)),
+            dma((NT // 2,)),
+            dma((NT // 2, 2)),
         ],
         compiler_params=pltpu.CompilerParams(
             collective_id=0, has_side_effects=True, vmem_limit_bytes=61 << 20

time: 121 us -> 111 us (0.917)
  Pallas kernels: 118 us -> 107 us
    pallas_call x1, Pallas kernels: 118 us -> 107 us  [layer(): pl.pallas_call(layer_kernel, name='layer', out_shape=jax.ShapeDtypeStruct...]
where the time goes in v3:
time: 111 us; the launch traced here: 109 us
  Pallas kernels  107 us (96%)
  other arithmetic  2.07 us (2%)
    pallas_call x1, Pallas kernels, layer(): pl.pallas_call(layer_kernel, name='layer', out_shape=jax.ShapeDtypeStruct...  107 us

profile of v3, /device:TPU:2, one launch (start us, length us, event | category | flops | bytes accessed | tf_op | source)
XLA Modules:
  0.0 109.4 jit_solution(13760448797479130439)
XLA Ops:
  0.0 107.3 %layer.1 = f32[64,4096]{1,0:T(8,128)} custom-call(s32[8,8]{1,0:T(8,128)} %lens.1, s32[8,8]{1,0:T(8,128)} %adap.1, s32[8]{0:T(128)} %aslot.1, bf16[64,4096]{1,0:T(8,128)(2,1)} %bitcast.8, bf16[4096,512]{1,0:T(8,128)(2,1)} %wq.1, bf16[4096,128]{1,0:T(8,128)(2,1)} %wk.1, bf16[4096,128]{1,0:T(8,128)(2,1)} %wv.1, bf16[512,4096]{1,0:T(8,128)(2,1)} %w_out.1, ...), custom_call_target="tpu_custom_call" | custom-call | tf_op jit(solution)/shard_map/layer/pallas_call | solution.py:615
  107.3 2.1 %convert_bitcast_fusion = bf16[1,64,4096]{2,1,0:T(8,128)(2,1)} fusion(f32[64,4096]{1,0:T(8,128)} %layer.1), kind=kLoop, calls=%fused_computation | loop fusion | flops 262144 | bytes 1572864 | tf_op jit(solution)/shard_map/broadcast_in_dim | solution.py:682

commit v4 on v3

--- a/solution.py
+++ b/solution.py
@@ -21,10 +21,10 @@
 
 QC = 512
 KVC = 128
-H = 4
+H = 2
 HR = 64 // H
 NR = 8 * HR
-NCH = 2
+NCH = 4
 KCH = D // NCH
 NJ = H * NCH
 LEAD = 4
@@ -533,7 +533,7 @@
         half = J // NN
         cols = pl.ds(pl.multiple_of((J % NN) * NC, NC), NC)
         total = sbuf[J, pc.y].astype(F32) + rup[J].astype(F32) + rdn[J].astype(F32)
-        out[pl.ds(pl.multiple_of(half * BR, BR), BR), cols] = total
+        out[pl.ds(pl.multiple_of(half * BR, BR), BR), cols] = total.astype(BF16)
 
     HP = NN // 2
 
@@ -551,9 +551,10 @@
             att_ready(0)
             mid_send(0)
 
-        @pl.when((it >= READY) & (it < READY + HP))
-        def _():
-            pair_p(it - READY)
+        @pl.when((it >= READY) & (it < READY + 4))
+        def _():
+            for i in range(HP // 4):
+                pair_p((it - READY) * (HP // 4) + i)
 
         return carry
 
@@ -615,7 +616,7 @@
     return pl.pallas_call(
         layer_kernel,
         name="layer",
-        out_shape=jax.ShapeDtypeStruct((64, D), F32),
+        out_shape=jax.ShapeDtypeStruct((64, D), BF16),
         in_specs=[smem] * 3 + [any_] * 10 + [vmem],
         out_specs=vmem,
         scratch_shapes=[
@@ -679,7 +680,7 @@
         req_lengths, req_adapter, adapter_slot, tokens[0], query_weight, key_weight, value_weight, w_out,
         down_qkv[0], up_query[0], up_kv[0], down_out[0], up_out[0], freq,
     )
-    return out.astype(BF16)[None]
+    return out[None]
 
 
 def solution(mesh):

time: 111 us -> 109 us (0.982); the launches traced: 109 us -> 109 us
  other arithmetic: 2.07 us -> 0 us
  local copies, waits for them, and re-layouts: 0 us -> 1.87 us
    broadcast_in_dim x1 -> x0, other arithmetic: 2.07 us -> none  [body(): return out.astype(BF16)[None]]
    unnamed x0 -> x1, local copies, waits for them, and re-layouts: none -> 1.87 us
where the time goes in v4:
time: 109 us
  Pallas kernels  107 us (98%)
  local copies, waits for them, and re-layouts  1.87 us (2%)
    pallas_call x1, Pallas kernels, layer(): pl.pallas_call(layer_kernel, name='layer', out_shape=jax.ShapeDtypeStruct...  107 us

profile of v4, /device:TPU:2, one launch (start us, length us, event | category | flops | bytes accessed | tf_op | source)
XLA Modules:
  0.0 108.8 jit_solution(10757738027623361128)
XLA Ops:
  0.0 106.9 %layer.1 = bf16[64,4096]{1,0:T(8,128)(2,1)} custom-call(s32[8,8]{1,0:T(8,128)} %lens.1, s32[8,8]{1,0:T(8,128)} %adap.1, s32[8]{0:T(128)} %aslot.1, bf16[64,4096]{1,0:T(8,128)(2,1)} %bitcast.8, bf16[4096,512]{1,0:T(8,128)(2,1)} %wq.1, bf16[4096,128]{1,0:T(8,128)(2,1)} %wk.1, bf16[4096,128]{1,0:T(8,128)(2,1)} %wv.1, bf16[512,4096]{1,0:T(8,128)(2,1)} %w_out.1, ...), custom_call_target="tpu_custom_call" | custom-call | tf_op jit(solution)/shard_map/layer/pallas_call | solution.py:616
  106.9 1.9 %copy.16 = bf16[1,64,4096]{2,1,0:T(8,128)(2,1)} copy(bf16[1,64,4096]{2,1,0:T(8,128)(2,1)} %bitcast.7) | data formatting | bytes 1048576
